TPU v7x, 512 devices: a whole 4x8x8 slice. The times are simulated.
512 devices in a mesh: seq: 128 (over z, y, core), head: 4 (over x).
Axes of the slice: x: 4, y: 8, z: 8, core: 2. Of those that a mesh axis runs over, the one named last changes fastest.
Arguments:
- query_rows: bfloat16 [16384, 2048], P('seq', 'head'), may hold values from -10 to 10
- key_rows: bfloat16 [16384, 2048], P('seq', 'head'), may hold values from -10 to 10
- value_rows: bfloat16 [16384, 2048], P('seq', 'head'), may hold values from -6 to 6
- out_weight: bfloat16 [2048, 2048], P('head'), may hold values from -0.1875 to 0.1875
- cluster_ids: int32 [128, 16], P('seq'), may hold values from 0 to 127, as said below
Outputs:
- layer_out: bfloat16 [16384, 2048], P('seq', 'head')
Inputs may be any that keep to these rules, and one draw needn't show every extreme that they name: `cluster_ids`: row d names the clusters of device d's blocks in order. One device names one cluster for at most 1 of its blocks; some cluster is named 1 times by every device, so its owner receives the most from every source. Cluster sizes are skewed.
All inputs are finite; a program needn't handle non-finite values.
Results may differ from a plain program's by a relative error of at most 0.01.
Values may be sent and summed in bfloat16 or wider, within the bound.
A program may use at most 64 MiB of HBM per device.

v0:
```python
import jax
import jax.numpy as jnp
from jax import lax
from jax.sharding import Mesh
from jax.sharding import PartitionSpec as P

HD = 128
WINDOW = 1024
SEQ = ("seq_0", "seq_1", "seq_2")


def joined_along(tiles, dim):
    tiles = jnp.moveaxis(tiles, 0, dim)
    dims = tiles.shape
    return tiles.reshape(*dims[:dim], dims[dim] * dims[dim + 1], *dims[dim + 2 :])


def all_blocks(value, axes, order):
    tiles = value[None]
    for k in order:
        tiles = lax.all_gather(tiles, axes[k], axis=0, tiled=True)
    carried = [lax.axis_size(axes[k]) for k in reversed(order)]
    tiles = tiles.reshape(*carried, *value.shape)
    turned = sorted(range(len(order)), key=lambda place: order[len(order) - 1 - place])
    return tiles.transpose(*turned, *range(len(order), tiles.ndim)).reshape(-1, *value.shape)


def gather_axes(value, axes, order, dim):
    return joined_along(all_blocks(value, axes, order), dim)


def in_blocks(value, dim, count):
    dims = value.shape
    tiles = value.reshape(*dims[:dim], count, dims[dim] // count, *dims[dim + 1 :])
    return jnp.moveaxis(tiles, dim, 0)


def exchange_in_order(tiles, axes, order):
    dims = [lax.axis_size(a) for a in axes]
    tiles = tiles.reshape(*dims, *tiles.shape[1:])
    for k in order:
        tiles = lax.all_to_all(tiles, axes[k], split_axis=k, concat_axis=k, tiled=True)
    return tiles.reshape(-1, *tiles.shape[len(axes) :])


def core_and_chips(value, groups, order, split_dim, concat_dim):
    count = lax.axis_size(groups[0]) * lax.axis_size(groups[1])
    tiles = in_blocks(value, split_dim, count)
    return joined_along(exchange_in_order(tiles, groups, order), concat_dim)


def shifted(value, axis, by):
    count = lax.axis_size(axis)
    pairs = [(i, i + by) for i in range(count) if 0 <= i + by < count]
    return lax.ppermute(value, axis, pairs)


def attend(queries_h, keys_h, values_h, allowed):
    scores = jnp.einsum(
        "qhd,khd->hqk", queries_h, keys_h, preferred_element_type=jnp.float32
    ) * queries_h.shape[2] ** (-0.5)
    scores = jnp.where(allowed[None], scores, -1e30)
    largest = jnp.max(scores, axis=2, keepdims=True)
    weights_raw = jnp.where(allowed[None], jnp.exp(scores - largest), 0.0)
    weights = (weights_raw / jnp.sum(weights_raw, axis=2, keepdims=True)).astype(jnp.bfloat16)
    return jnp.einsum("hqk,khd->qhd", weights, values_h, preferred_element_type=jnp.float32)


def owner_attend(arrived_q, arrived_k, arrived_v, positions, present):
    total_rows = arrived_q.shape[0]
    results = []
    for first_row in range(0, total_rows, 512):
        last_row = min(first_row + 512, total_rows)
        query_pos = positions[first_row:last_row]
        key_pos = positions[:last_row]
        self_mask = jnp.arange(first_row, last_row)[:, None] == jnp.arange(last_row)[None, :]
        allowed = present[None, :last_row] & (key_pos[None, :] <= query_pos[:, None]) | self_mask
        output_rows = attend(
            arrived_q[first_row:last_row], arrived_k[:last_row], arrived_v[:last_row], allowed
        )
        results.append(output_rows.astype(jnp.bfloat16))
    return jnp.concatenate(results, axis=0)


def flatten_rows(array_in):
    return array_in.reshape(-1, array_in.shape[3], array_in.shape[4])


def body(query_rows, key_rows, value_rows, out_weight, cluster_ids):
    seq_count = lax.axis_size(SEQ)
    seq_index = lax.axis_index(SEQ)
    tok_dev = query_rows.shape[0]
    blocks_here = cluster_ids.shape[1]
    block_rows = tok_dev // blocks_here
    head_dim = HD
    heads_here = query_rows.shape[1] // head_dim
    slot_count = -(-blocks_here // seq_count)
    own_ids = cluster_ids[0]
    block_iota = jnp.arange(blocks_here, dtype=jnp.int32)
    same_cluster = own_ids[:, None] == own_ids[None, :]
    own_rank = jnp.sum(same_cluster & (block_iota[None, :] < block_iota[:, None]), axis=1)
    dest_slot = own_ids * slot_count + own_rank
    slot_iota = jnp.arange(seq_count * slot_count, dtype=jnp.int32)
    slot_hits = dest_slot[None, :] == slot_iota[:, None]
    source_block = jnp.where(
        jnp.any(slot_hits, axis=1),
        jnp.sum(jnp.where(slot_hits, block_iota[None, :], 0), axis=1),
        blocks_here,
    )

    def to_slots(rows_in):
        blocked = rows_in.reshape(blocks_here, block_rows, heads_here, head_dim)
        picked = jnp.take(blocked, source_block, axis=0, mode="fill", fill_value=0)
        return picked.reshape(seq_count, slot_count, block_rows, heads_here, head_dim)

    all_ids = gather_axes(cluster_ids, (("seq_0", "seq_1"), "seq_2"), (0, 1), 0)
    matches = (all_ids == seq_index).astype(jnp.int32)
    earlier = jnp.cumsum(matches, axis=1) - matches
    slot_match = (matches[:, None, :] == 1) & (
        earlier[:, None, :] == jnp.arange(slot_count, dtype=jnp.int32)[None, :, None]
    )
    present_slot = jnp.any(slot_match, axis=2)
    block_of_slot = jnp.sum(jnp.where(slot_match, block_iota[None, None, :], 0), axis=2)
    start_pos = (
        jnp.arange(seq_count, dtype=jnp.int32)[:, None] * blocks_here + block_of_slot
    ) * block_rows
    positions = (
        start_pos[:, :, None] + jnp.arange(block_rows, dtype=jnp.int32)[None, None, :]
    ).reshape(-1)
    present = jnp.broadcast_to(
        present_slot[:, :, None], (seq_count, slot_count, block_rows)
    ).reshape(-1)
    arrived_q = lax.all_to_all(to_slots(query_rows), SEQ, split_axis=0, concat_axis=0, tiled=True)
    arrived_k = lax.all_to_all(to_slots(key_rows), SEQ, split_axis=0, concat_axis=0, tiled=True)
    arrived_v = lax.all_to_all(to_slots(value_rows), SEQ, split_axis=0, concat_axis=0, tiled=True)
    heads_now = arrived_q.shape[3]
    result = owner_attend(
        flatten_rows(arrived_q),
        flatten_rows(arrived_k),
        flatten_rows(arrived_v),
        positions,
        present,
    )
    result = result.reshape(seq_count, slot_count, block_rows, heads_now, head_dim)
    returned = core_and_chips(result, (("seq_0", "seq_1"), "seq_2"), (1, 0), 0, 0)
    returned = returned.reshape(seq_count * slot_count, block_rows, heads_here, head_dim)
    routed_here = jnp.take(returned, dest_slot, axis=0).reshape(tok_dev, heads_here, head_dim)
    shard_reach = WINDOW // tok_dev
    key_parts = [key_rows]
    value_parts = [value_rows]
    carried_k, carried_v = (key_rows, value_rows)
    for reach_step in range(shard_reach):
        carried_k, carried_v = shifted((carried_k, carried_v), SEQ, 1)
        key_parts.insert(0, carried_k)
        value_parts.insert(0, carried_v)
    near_k = jnp.concatenate(key_parts, axis=0).reshape(-1, heads_here, head_dim)
    near_v = jnp.concatenate(value_parts, axis=0).reshape(-1, heads_here, head_dim)
    queries_local = query_rows.reshape(tok_dev, heads_here, head_dim)
    last_query = min(512, tok_dev)
    query_pos = jnp.arange(0, last_query, dtype=jnp.int32)[:, None]
    key_rel = jnp.arange(0, last_query + WINDOW, dtype=jnp.int32)[None, :] - WINDOW
    allowed = (
        (key_rel <= query_pos)
        & (key_rel > query_pos - WINDOW)
        & (seq_index * tok_dev + key_rel >= 0)
    )
    local_blocks = attend(queries_local, near_k, near_v, allowed)
    attended = (
        (routed_here.astype(jnp.float32) + local_blocks)
        .astype(jnp.bfloat16)
        .reshape(tok_dev, heads_here * head_dim)
    )
    weight_cols = lax.all_to_all(out_weight, "head", split_axis=1, concat_axis=0, tiled=True)
    summed = jnp.dot(
        lax.all_gather(attended, "head", axis=1, tiled=True),
        weight_cols,
        preferred_element_type=jnp.float32,
    )
    return summed.astype(jnp.bfloat16)


def solution(mesh):
    split = Mesh(
        mesh.devices.reshape(8, 8, 2, mesh.shape["head"]), ("seq_0", "seq_1", "seq_2", "head")
    )
    return jax.shard_map(
        body,
        mesh=split,
        in_specs=(P(SEQ, "head"), P(SEQ, "head"), P(SEQ, "head"), P("head", None), P(SEQ, None)),
        out_specs=P(SEQ, "head"),
        check_vma=False,
    )
```

profile of v0, /device:TPU:1, one launch (start us, length us, event | category | flops | bytes accessed | tf_op | source)
XLA Modules:
  0.0 296.5 jit_solution(10110788097195472716)
XLA Ops:
  1.8 1.7 gather_fusion.1
  5.1 2.0 select_bitcast_fusion.2
  7.0 18.5 %all-to-all-start.1 = ((bf16[128,1,8,4,128]{4,2,3,1,0:T(8,128)(2,1)}), bf16[128,1,8,4,128]{4,2,3,1,0:T(8,128)(2,1)S(1)}, u32[]{:S(2)}, u32[]{:S(2)}) async-start(bf16[128,1,8,4,128]{4,2,3,1,0:T(8,128)(2,1)} %get-tuple-element.15), calls=%async_computation.1 | async-start | bytes 2097152 | tf_op jit(solution)/shard_map/all_to_all | solution.py:133
  25.6 3.5 %collective-permute-start = (bf16[128,512]{1,0:T(8,128)(2,1)S(1)}, bf16[128,512]{1,0:T(8,128)(2,1)S(1)}, u32[]{:S(2)}, u32[]{:S(2)}) collective-permute-start(bf16[128,512]{1,0:T(8,128)(2,1)S(1)} %copy-done.2), channel_id=1, source_target_pairs={{0,4},{4,8},{8,12},{12,16},{16,20},{20,24},{24,28},{28,32},{32,36}... | collective-permute-start | bytes 393224 | tf_op jit(solution)/shard_map/ppermute | solution.py:55
  29.3 2.0 collective-permute-start.8
  31.3 50.6 %all-gather.2 = s32[64,1,16]{2,1,0:T(1,128)S(1)} all-gather(s32[1,1,16]{2,1,0:T(1,128)S(1)} %bitcast.133), channel_id=2, replica_groups=mesh['seq_0'=8,'seq_1'=8,'seq_2'=2,'head'=4] {'seq_0','seq_1'}, dimensions={0}, use_global_device_ids=true | all-gather | bytes 4160 | tf_op jit(solution)/shard_map/all_gather | solution.py:21
  82.0 8.8 %all-gather.3 = s32[2,64,16]{1,2,0:T(8,128)S(1)} all-gather(s32[1,64,16]{1,2,0:T(8,128)S(1)} %copy.117), channel_id=3, replica_groups=mesh['seq_0'=8,'seq_1'=8,'seq_2'=2,'head'=4] {'seq_2'}, dimensions={0}, use_global_device_ids=true | all-gather | bytes 12288 | tf_op jit(solution)/shard_map/all_gather | solution.py:21
  91.4 9.5 %all-to-all-start.2 = ((bf16[128,1,8,4,128]{4,2,3,1,0:T(8,128)(2,1)}), bf16[128,1,8,4,128]{4,2,3,1,0:T(8,128)(2,1)S(1)}, u32[]{:S(2)}, u32[]{:S(2)}) async-start(bf16[128,1,8,4,128]{4,2,3,1,0:T(8,128)(2,1)} %get-tuple-element.16), calls=%async_computation.2 | async-start | bytes 2097152 | tf_op jit(solution)/shard_map/all_to_all | solution.py:134
  102.5 3.9 %copy.147 = bf16[512,2048]{0,1:T(8,128)(2,1)} copy(bf16[512,2048]{1,0:T(8,128)(2,1)} %param.10) | data formatting | bytes 4194304 | tf_op args[3]
  106.4 3.5 %collective-permute-start.1 = (bf16[128,512]{1,0:T(8,128)(2,1)S(1)}, bf16[128,512]{1,0:T(8,128)(2,1)S(1)}, u32[]{:S(2)}, u32[]{:S(2)}) collective-permute-start(bf16[128,512]{1,0:T(8,128)(2,1)S(1)} %collective-permute-done), channel_id=1, source_target_pairs={{0,4},{4,8},{8,12},{12,16},{16,20},{20,24},{24,28},{28,32},{32,36}... | collective-permute-start | bytes 393224 | tf_op jit(solution)/shard_map/ppermute | solution.py:55
  111.5 2.0 collective-permute-start.9
  113.5 10.4 %collective-permute-done.1 = bf16[128,512]{1,0:T(8,128)(2,1)S(1)} collective-permute-done((bf16[128,512]{1,0:T(8,128)(2,1)S(1)}, bf16[128,512]{1,0:T(8,128)(2,1)S(1)}, u32[]{:S(2)}, u32[]{:S(2)}) %collective-permute-start.1) | collective-permute-done | bytes 131104 | tf_op jit(solution)/shard_map/ppermute | solution.py:55
  123.9 4.4 %collective-permute-start.2 = (bf16[128,512]{1,0:T(8,128)(2,1)S(1)}, bf16[128,512]{1,0:T(8,128)(2,1)}, u32[]{:S(2)}, u32[]{:S(2)}) collective-permute-start(bf16[128,512]{1,0:T(8,128)(2,1)S(1)} %collective-permute-done.1), channel_id=1, source_target_pairs={{0,4},{4,8},{8,12},{12,16},{16,20},{20,24},{24,28},{28,32},{32,36}... | collective-permute-start | bytes 393224 | tf_op jit(solution)/shard_map/ppermute | solution.py:55
  129.3 1.9 collective-permute-start.10
  131.2 4.0 %collective-permute-start.3 = (bf16[128,512]{1,0:T(8,128)(2,1)}, bf16[128,512]{1,0:T(8,128)(2,1)}, u32[]{:S(2)}, u32[]{:S(2)}) collective-permute-start(bf16[128,512]{1,0:T(8,128)(2,1)} %collective-permute-done.2), channel_id=1, source_target_pairs={{0,4},{4,8},{8,12},{12,16},{16,20},{20,24},{24,28},{28,32},{32,36}... | collective-permute-start | bytes 393224 | tf_op jit(solution)/shard_map/ppermute | solution.py:55
  135.3 15.4 %all-to-all-start = ((bf16[128,1,8,4,128]{4,2,3,1,0:T(8,128)(2,1)}), bf16[128,1,8,4,128]{4,2,3,1,0:T(8,128)(2,1)S(1)}, u32[]{:S(2)}, u32[]{:S(2)}) async-start(bf16[128,1,8,4,128]{4,2,3,1,0:T(8,128)(2,1)} %get-tuple-element.14), calls=%async_computation | async-start | bytes 2097152 | tf_op jit(solution)/shard_map/all_to_all | solution.py:135
  152.7 4.1 %fusion.68 = (f32[4,512]{1,0:T(4,128)S(1)}, f32[4,512,512]{1,2,0:T(8,128)}) fusion(f32[4,512,512]{1,2,0:T(8,128)S(1)} %fusion.35, pred[512,512]{0,1:T(8,128)(4,1)S(1)} %copy-done.5), kind=kOutput, calls=%fused_computation.124 | output fusion | flops 7340543 | bytes 8658944 | tf_op jit(solution)/shard_map/sub | solution.py:64
  156.9 6.4 %fusion.67 = (f32[4,512]{1,0:T(4,128)S(1)}, f32[4,512,1024]{2,1,0:T(8,128)}) fusion(f32[4,512,1024]{2,1,0:T(8,128)S(1)} %fusion.27, pred[512,1024]{1,0:T(8,128)(4,1)S(1)} %copy-done.4), kind=kOutput, calls=%fused_computation.123 | output fusion | flops 14681087 | bytes 17309696 | tf_op jit(solution)/shard_map/sub | solution.py:64
  163.3 18.4 %all-to-all-done = bf16[128,1,8,4,128]{4,2,3,1,0:T(8,128)(2,1)S(1)} async-done(((bf16[128,1,8,4,128]{4,2,3,1,0:T(8,128)(2,1)}), bf16[128,1,8,4,128]{4,2,3,1,0:T(8,128)(2,1)S(1)}, u32[]{:S(2)}, u32[]{:S(2)}) %all-to-all-start) | async-done | bytes 1048608 | tf_op jit(solution)/shard_map/all_to_all | solution.py:135
  181.7 2.9 fusion.22
  184.6 1.8 copy-done.16
  186.3 1.9 fusion.21
  189.3 4.3 %all_to_all.44 = bf16[64,2,1,1,8,4,128]{6,4,0,5,3,2,1:T(8,128)(2,1)S(1)} all-to-all(bf16[64,2,1,1,8,4,128]{6,4,0,5,3,2,1:T(8,128)(2,1)S(1)} %copy.136), channel_id=1, replica_groups=mesh['seq_0'=8,'seq_1'=8,'seq_2'=2,'head'=4] {'seq_2'}, dimensions={1} | all-to-all | bytes 2097152 | tf_op jit(solution)/shard_map/all_to_all | solution.py:42
  193.6 4.0 %all-to-all-start.5 = ((bf16[512,4,512]{0,2,1:T(8,128)(2,1)}), bf16[512,4,512]{0,2,1:T(8,128)(2,1)S(1)}, u32[]{:S(2)}, u32[]{:S(2)}) async-start(bf16[512,4,512]{0,2,1:T(8,128)(2,1)} %bitcast.36), calls=%async_computation.5 | async-start | bytes 4194304 | tf_op jit(solution)/shard_map/all_to_all | solution.py:173
  197.7 4.5 %collective-permute-start.11 = (bf16[128,512]{0,1:T(8,128)(2,1)}, bf16[128,512]{0,1:T(8,128)(2,1)S(1)}, u32[]{:S(2)}, u32[]{:S(2)}) collective-permute-start(bf16[128,512]{0,1:T(8,128)(2,1)} %collective-permute-done.10), channel_id=1, source_target_pairs={{0,4},{4,8},{8,12},{12,16},{16,20},{20,24},{24,28},{28,32},{32,36}... | collective-permute-start | bytes 393224 | tf_op jit(solution)/shard_map/ppermute | solution.py:55
  202.2 1.9 collective-permute-start.4
  205.1 4.2 %collective-permute-start.12 = (bf16[128,512]{0,1:T(8,128)(2,1)S(1)}, bf16[128,512]{0,1:T(8,128)(2,1)S(1)}, u32[]{:S(2)}, u32[]{:S(2)}) collective-permute-start(bf16[128,512]{0,1:T(8,128)(2,1)S(1)} %collective-permute-done.11), channel_id=1, source_target_pairs={{0,4},{4,8},{8,12},{12,16},{16,20},{20,24},{24,28},{28,32},{32,36}... | collective-permute-start | bytes 393224 | tf_op jit(solution)/shard_map/ppermute | solution.py:55
  209.3 1.9 collective-permute-start.5
  213.4 2.8 collective-permute-start.13
  216.3 1.9 collective-permute-start.6
  218.2 4.4 %collective-permute-start.14 = (bf16[128,512]{0,1:T(8,128)(2,1)}, bf16[128,512]{0,1:T(8,128)(2,1)}, u32[]{:S(2)}, u32[]{:S(2)}) collective-permute-start(bf16[128,512]{0,1:T(8,128)(2,1)} %collective-permute-done.13), channel_id=1, source_target_pairs={{0,4},{4,8},{8,12},{12,16},{16,20},{20,24},{24,28},{28,32},{32,36}... | collective-permute-start | bytes 393224 | tf_op jit(solution)/shard_map/ppermute | solution.py:55
  222.7 1.9 collective-permute-start.7
  224.9 4.3 %collective-permute-start.15 = (bf16[128,512]{0,1:T(8,128)(2,1)}, bf16[128,512]{0,1:T(8,128)(2,1)}, u32[]{:S(2)}, u32[]{:S(2)}) collective-permute-start(bf16[128,512]{0,1:T(8,128)(2,1)} %collective-permute-done.14), channel_id=1, source_target_pairs={{0,4},{4,8},{8,12},{12,16},{16,20},{20,24},{24,28},{28,32},{32,36}... | collective-permute-start | bytes 393224 | tf_op jit(solution)/shard_map/ppermute | solution.py:55
  229.2 1.6 constant_dynamic-update-slice_fusion.8
  230.8 1.6 constant_dynamic-update-slice_fusion.7
  233.7 17.9 %all-to-all-start.4 = ((bf16[64,2,1,1,8,4,128]{6,4,1,5,3,2,0:T(8,128)(2,1)}), bf16[64,2,1,1,8,4,128]{6,4,1,5,3,2,0:T(8,128)(2,1)S(1)}, u32[]{:S(2)}, u32[]{:S(2)}) async-start(bf16[64,2,1,1,8,4,128]{6,4,1,5,3,2,0:T(8,128)(2,1)} %copy.137), calls=%async_computation.4 | async-start | bytes 2097152 | tf_op jit(solution)/shard_map/all_to_all | solution.py:42
  251.6 1.6 constant_dynamic-update-slice_fusion.6
  253.2 1.5 constant_dynamic-update-slice_fusion.5
  254.8 1.6 constant_dynamic-update-slice_fusion.4
  256.3 1.6 constant_dynamic-update-slice_fusion.3
  257.9 1.6 constant_dynamic-update-slice_fusion.2
  259.4 1.6 constant_dynamic-update-slice_fusion.1
  261.7 2.4 copy.141
  271.8 4.0 %fusion.64 = (f32[4,128]{1,0:T(4,128)S(1)}, f32[4,128,1152]{1,2,0:T(8,128)}) fusion(bf16[1152,4,128]{0,2,1:T(8,128)(2,1)} %bitcast.130, pred[128,1152]{0,1:T(8,128)(4,1)} %fusion.33, bf16[128,512]{1,0:T(8,128)(2,1)S(1)} %copy-done), kind=kOutput, calls=%fused_computation.122 | convolution fusion | flops 153945216 | bytes 3819520 | tf_op jit(solution)/shard_map/sub | solution.py:64
  275.8 2.4 copy.148
  278.1 1.8 all-to-all-done.4
  280.9 2.6 fusion.26
  283.6 11.7 %all_gather.11 = bf16[128,2048]{0,1:T(8,128)(2,1)S(1)} all-gather(bf16[128,512]{0,1:T(8,128)(2,1)S(1)} %bitcast.128), channel_id=1, replica_groups=mesh['seq_0'=8,'seq_1'=8,'seq_2'=2,'head'=4] {'head'}, dimensions={1}, use_global_device_ids=true | all-gather | bytes 655360 | tf_op jit(solution)/shard_map/all_gather | solution.py:175
  (118 shorter events, 26.2 us)
Async XLA Ops:
  0.0 3.5 %copy-start = (bf16[128,512]{1,0:T(8,128)(2,1)S(1)}, bf16[128,512]{1,0:T(8,128)(2,1)}, u32[]{:S(2)}) copy-start(bf16[128,512]{1,0:T(8,128)(2,1)} %param.7) | copy-start | bytes 393220
  1.8 2.5 copy-start.1
  7.0 18.6 %copy-start.2 = (bf16[128,512]{1,0:T(8,128)(2,1)S(1)}, bf16[128,512]{1,0:T(8,128)(2,1)}, u32[]{:S(2)}) copy-start(bf16[128,512]{1,0:T(8,128)(2,1)} %param.9) | copy-start | bytes 393220
  7.0 24.3 %copy-start.15 = (s32[1,16]{1,0:T(1,128)S(1)}, s32[1,16]{1,0:T(1,128)}, u32[]{:S(2)}) copy-start(s32[1,16]{1,0:T(1,128)} %param.11) | copy-start | bytes 196
  7.0 84.4 %all-to-all-start.1 = ((bf16[128,1,8,4,128]{4,2,3,1,0:T(8,128)(2,1)}), bf16[128,1,8,4,128]{4,2,3,1,0:T(8,128)(2,1)S(1)}, u32[]{:S(2)}, u32[]{:S(2)}) async-start(bf16[128,1,8,4,128]{4,2,3,1,0:T(8,128)(2,1)} %get-tuple-element.15), calls=%async_computation.1 | async-start | bytes 2097152 | tf_op jit(solution)/shard_map/all_to_all | solution.py:133
  25.6 80.9 %collective-permute-start = (bf16[128,512]{1,0:T(8,128)(2,1)S(1)}, bf16[128,512]{1,0:T(8,128)(2,1)S(1)}, u32[]{:S(2)}, u32[]{:S(2)}) collective-permute-start(bf16[128,512]{1,0:T(8,128)(2,1)S(1)} %copy-done.2), channel_id=1, source_target_pairs={{0,4},{4,8},{8,12},{12,16},{16,20},{20,24},{24,28},{28,32},{32,36}... | collective-permute-start | bytes 393224 | tf_op jit(solution)/shard_map/ppermute | solution.py:55
  29.3 82.2 %collective-permute-start.8 = (bf16[128,512]{0,1:T(8,128)(2,1)S(1)}, bf16[128,512]{0,1:T(8,128)(2,1)S(1)}, u32[]{:S(2)}, u32[]{:S(2)}) collective-permute-start(bf16[128,512]{0,1:T(8,128)(2,1)S(1)} %copy.142), channel_id=1, source_target_pairs={{0,4},{4,8},{8,12},{12,16},{16,20},{20,24},{24,28},{28,32},{32,36}... | collective-permute-start | bytes 393224 | tf_op jit(solution)/shard_map/ppermute | solution.py:55
  91.4 43.9 %all-to-all-start.2 = ((bf16[128,1,8,4,128]{4,2,3,1,0:T(8,128)(2,1)}), bf16[128,1,8,4,128]{4,2,3,1,0:T(8,128)(2,1)S(1)}, u32[]{:S(2)}, u32[]{:S(2)}) async-start(bf16[128,1,8,4,128]{4,2,3,1,0:T(8,128)(2,1)} %get-tuple-element.16), calls=%async_computation.2 | async-start | bytes 2097152 | tf_op jit(solution)/shard_map/all_to_all | solution.py:134
  106.4 24.8 %copy-start.8 = (bf16[128,512]{1,0:T(8,128)(2,1)}, bf16[128,512]{1,0:T(8,128)(2,1)S(1)}, u32[]{:S(2)}) copy-start(bf16[128,512]{1,0:T(8,128)(2,1)S(1)} %collective-permute-done) | copy-start | bytes 393220
  106.4 17.5 %collective-permute-start.1 = (bf16[128,512]{1,0:T(8,128)(2,1)S(1)}, bf16[128,512]{1,0:T(8,128)(2,1)S(1)}, u32[]{:S(2)}, u32[]{:S(2)}) collective-permute-start(bf16[128,512]{1,0:T(8,128)(2,1)S(1)} %collective-permute-done), channel_id=1, source_target_pairs={{0,4},{4,8},{8,12},{12,16},{16,20},{20,24},{24,28},{28,32},{32,36}... | collective-permute-start | bytes 393224 | tf_op jit(solution)/shard_map/ppermute | solution.py:55
  111.5 19.7 %copy-start.6 = (bf16[128,512]{0,1:T(8,128)(2,1)}, bf16[128,512]{0,1:T(8,128)(2,1)S(1)}, u32[]{:S(2)}) copy-start(bf16[128,512]{0,1:T(8,128)(2,1)S(1)} %collective-permute-done.8) | copy-start | bytes 393220
  111.5 17.8 %collective-permute-start.9 = (bf16[128,512]{0,1:T(8,128)(2,1)S(1)}, bf16[128,512]{0,1:T(8,128)(2,1)}, u32[]{:S(2)}, u32[]{:S(2)}) collective-permute-start(bf16[128,512]{0,1:T(8,128)(2,1)S(1)} %collective-permute-done.8), channel_id=1, source_target_pairs={{0,4},{4,8},{8,12},{12,16},{16,20},{20,24},{24,28},{28,32},{32,36}... | collective-permute-start | bytes 393224 | tf_op jit(solution)/shard_map/ppermute | solution.py:55
  123.9 7.3 %copy-start.9 = (bf16[128,512]{1,0:T(8,128)(2,1)}, bf16[128,512]{1,0:T(8,128)(2,1)S(1)}, u32[]{:S(2)}) copy-start(bf16[128,512]{1,0:T(8,128)(2,1)S(1)} %collective-permute-done.1) | copy-start | bytes 393220
  123.9 7.3 %collective-permute-start.2 = (bf16[128,512]{1,0:T(8,128)(2,1)S(1)}, bf16[128,512]{1,0:T(8,128)(2,1)}, u32[]{:S(2)}, u32[]{:S(2)}) collective-permute-start(bf16[128,512]{1,0:T(8,128)(2,1)S(1)} %collective-permute-done.1), channel_id=1, source_target_pairs={{0,4},{4,8},{8,12},{12,16},{16,20},{20,24},{24,28},{28,32},{32,36}... | collective-permute-start | bytes 393224 | tf_op jit(solution)/shard_map/ppermute | solution.py:55
  129.3 68.4 %collective-permute-start.10 = (bf16[128,512]{0,1:T(8,128)(2,1)}, bf16[128,512]{0,1:T(8,128)(2,1)}, u32[]{:S(2)}, u32[]{:S(2)}) collective-permute-start(bf16[128,512]{0,1:T(8,128)(2,1)} %collective-permute-done.9), channel_id=1, source_target_pairs={{0,4},{4,8},{8,12},{12,16},{16,20},{20,24},{24,28},{28,32},{32,36}... | collective-permute-start | bytes 393224 | tf_op jit(solution)/shard_map/ppermute | solution.py:55
  131.2 71.0 %collective-permute-start.3 = (bf16[128,512]{1,0:T(8,128)(2,1)}, bf16[128,512]{1,0:T(8,128)(2,1)}, u32[]{:S(2)}, u32[]{:S(2)}) collective-permute-start(bf16[128,512]{1,0:T(8,128)(2,1)} %collective-permute-done.2), channel_id=1, source_target_pairs={{0,4},{4,8},{8,12},{12,16},{16,20},{20,24},{24,28},{28,32},{32,36}... | collective-permute-start | bytes 393224 | tf_op jit(solution)/shard_map/ppermute | solution.py:55
  135.3 46.4 %all-to-all-start = ((bf16[128,1,8,4,128]{4,2,3,1,0:T(8,128)(2,1)}), bf16[128,1,8,4,128]{4,2,3,1,0:T(8,128)(2,1)S(1)}, u32[]{:S(2)}, u32[]{:S(2)}) async-start(bf16[128,1,8,4,128]{4,2,3,1,0:T(8,128)(2,1)} %get-tuple-element.14), calls=%async_computation | async-start | bytes 2097152 | tf_op jit(solution)/shard_map/all_to_all | solution.py:135
  151.4 1.3 copy-start.5
  152.7 4.2 %copy-start.4 = (pred[512,1024]{1,0:T(8,128)(4,1)S(1)}, pred[512,1024]{1,0:T(8,128)(4,1)}, u32[]{:S(2)}) copy-start(pred[512,1024]{1,0:T(8,128)(4,1)} %fusion.17) | copy-start | bytes 1572868
  181.7 4.6 %copy-start.16 = (f32[4,512,1024]{2,1,0:T(8,128)S(1)}, f32[4,512,1024]{2,1,0:T(8,128)}, u32[]{:S(2)}) copy-start(f32[4,512,1024]{2,1,0:T(8,128)} %get-tuple-element.20) | copy-start | bytes 25165828
  193.6 40.1 %all-to-all-start.5 = ((bf16[512,4,512]{0,2,1:T(8,128)(2,1)}), bf16[512,4,512]{0,2,1:T(8,128)(2,1)S(1)}, u32[]{:S(2)}, u32[]{:S(2)}) async-start(bf16[512,4,512]{0,2,1:T(8,128)(2,1)} %bitcast.36), calls=%async_computation.5 | async-start | bytes 4194304 | tf_op jit(solution)/shard_map/all_to_all | solution.py:173
  197.7 6.8 %collective-permute-start.11 = (bf16[128,512]{0,1:T(8,128)(2,1)}, bf16[128,512]{0,1:T(8,128)(2,1)S(1)}, u32[]{:S(2)}, u32[]{:S(2)}) collective-permute-start(bf16[128,512]{0,1:T(8,128)(2,1)} %collective-permute-done.10), channel_id=1, source_target_pairs={{0,4},{4,8},{8,12},{12,16},{16,20},{20,24},{24,28},{28,32},{32,36}... | collective-permute-start | bytes 393224 | tf_op jit(solution)/shard_map/ppermute | solution.py:55
  202.2 7.1 %collective-permute-start.4 = (bf16[128,512]{1,0:T(8,128)(2,1)}, bf16[128,512]{1,0:T(8,128)(2,1)S(1)}, u32[]{:S(2)}, u32[]{:S(2)}) collective-permute-start(bf16[128,512]{1,0:T(8,128)(2,1)} %collective-permute-done.3), channel_id=1, source_target_pairs={{0,4},{4,8},{8,12},{12,16},{16,20},{20,24},{24,28},{28,32},{32,36}... | collective-permute-start | bytes 393224 | tf_op jit(solution)/shard_map/ppermute | solution.py:55
  204.4 0.6 copy-start.10
  205.1 7.7 %collective-permute-start.12 = (bf16[128,512]{0,1:T(8,128)(2,1)S(1)}, bf16[128,512]{0,1:T(8,128)(2,1)S(1)}, u32[]{:S(2)}, u32[]{:S(2)}) collective-permute-start(bf16[128,512]{0,1:T(8,128)(2,1)S(1)} %collective-permute-done.11), channel_id=1, source_target_pairs={{0,4},{4,8},{8,12},{12,16},{16,20},{20,24},{24,28},{28,32},{32,36}... | collective-permute-start | bytes 393224 | tf_op jit(solution)/shard_map/ppermute | solution.py:55
  209.3 8.9 %copy-start.12 = (bf16[128,512]{1,0:T(8,128)(2,1)}, bf16[128,512]{1,0:T(8,128)(2,1)S(1)}, u32[]{:S(2)}) copy-start(bf16[128,512]{1,0:T(8,128)(2,1)S(1)} %collective-permute-done.4) | copy-start | bytes 393220
  209.3 6.9 %collective-permute-start.5 = (bf16[128,512]{1,0:T(8,128)(2,1)S(1)}, bf16[128,512]{1,0:T(8,128)(2,1)S(1)}, u32[]{:S(2)}, u32[]{:S(2)}) collective-permute-start(bf16[128,512]{1,0:T(8,128)(2,1)S(1)} %collective-permute-done.4), channel_id=1, source_target_pairs={{0,4},{4,8},{8,12},{12,16},{16,20},{20,24},{24,28},{28,32},{32,36}... | collective-permute-start | bytes 393224 | tf_op jit(solution)/shard_map/ppermute | solution.py:55
  212.8 0.7 copy-start.11
  213.4 4.8 %collective-permute-start.13 = (bf16[128,512]{0,1:T(8,128)(2,1)S(1)}, bf16[128,512]{0,1:T(8,128)(2,1)}, u32[]{:S(2)}, u32[]{:S(2)}) collective-permute-start(bf16[128,512]{0,1:T(8,128)(2,1)S(1)} %collective-permute-done.12), channel_id=1, source_target_pairs={{0,4},{4,8},{8,12},{12,16},{16,20},{20,24},{24,28},{28,32},{32,36}... | collective-permute-start | bytes 393224 | tf_op jit(solution)/shard_map/ppermute | solution.py:55
  216.3 6.4 %copy-start.13 = (bf16[128,512]{1,0:T(8,128)(2,1)}, bf16[128,512]{1,0:T(8,128)(2,1)S(1)}, u32[]{:S(2)}) copy-start(bf16[128,512]{1,0:T(8,128)(2,1)S(1)} %collective-permute-done.5) | copy-start | bytes 393220
  216.3 6.4 %collective-permute-start.6 = (bf16[128,512]{1,0:T(8,128)(2,1)S(1)}, bf16[128,512]{1,0:T(8,128)(2,1)}, u32[]{:S(2)}, u32[]{:S(2)}) collective-permute-start(bf16[128,512]{1,0:T(8,128)(2,1)S(1)} %collective-permute-done.5), channel_id=1, source_target_pairs={{0,4},{4,8},{8,12},{12,16},{16,20},{20,24},{24,28},{28,32},{32,36}... | collective-permute-start | bytes 393224 | tf_op jit(solution)/shard_map/ppermute | solution.py:55
  218.2 6.6 %collective-permute-start.14 = (bf16[128,512]{0,1:T(8,128)(2,1)}, bf16[128,512]{0,1:T(8,128)(2,1)}, u32[]{:S(2)}, u32[]{:S(2)}) collective-permute-start(bf16[128,512]{0,1:T(8,128)(2,1)} %collective-permute-done.13), channel_id=1, source_target_pairs={{0,4},{4,8},{8,12},{12,16},{16,20},{20,24},{24,28},{28,32},{32,36}... | collective-permute-start | bytes 393224 | tf_op jit(solution)/shard_map/ppermute | solution.py:55
  222.7 6.6 %collective-permute-start.7 = (bf16[128,512]{1,0:T(8,128)(2,1)}, bf16[128,512]{1,0:T(8,128)(2,1)}, u32[]{:S(2)}, u32[]{:S(2)}) collective-permute-start(bf16[128,512]{1,0:T(8,128)(2,1)} %collective-permute-done.6), channel_id=1, source_target_pairs={{0,4},{4,8},{8,12},{12,16},{16,20},{20,24},{24,28},{28,32},{32,36}... | collective-permute-start | bytes 393224 | tf_op jit(solution)/shard_map/ppermute | solution.py:55
  224.9 39.2 %collective-permute-start.15 = (bf16[128,512]{0,1:T(8,128)(2,1)}, bf16[128,512]{0,1:T(8,128)(2,1)}, u32[]{:S(2)}, u32[]{:S(2)}) collective-permute-start(bf16[128,512]{0,1:T(8,128)(2,1)} %collective-permute-done.14), channel_id=1, source_target_pairs={{0,4},{4,8},{8,12},{12,16},{16,20},{20,24},{24,28},{28,32},{32,36}... | collective-permute-start | bytes 393224 | tf_op jit(solution)/shard_map/ppermute | solution.py:55
  233.7 46.3 %all-to-all-start.4 = ((bf16[64,2,1,1,8,4,128]{6,4,1,5,3,2,0:T(8,128)(2,1)}), bf16[64,2,1,1,8,4,128]{6,4,1,5,3,2,0:T(8,128)(2,1)S(1)}, u32[]{:S(2)}, u32[]{:S(2)}) async-start(bf16[64,2,1,1,8,4,128]{6,4,1,5,3,2,0:T(8,128)(2,1)} %copy.137), calls=%async_computation.4 | async-start | bytes 2097152 | tf_op jit(solution)/shard_map/all_to_all | solution.py:42
  261.7 9.0 %copy-start.7 = (bf16[128,512]{0,1:T(8,128)(2,1)S(1)}, bf16[128,512]{0,1:T(8,128)(2,1)}, u32[]{:S(2)}) copy-start(bf16[128,512]{0,1:T(8,128)(2,1)} %copy-done.6) | copy-start | bytes 393220
  270.8 1.0 copy-start.14
  280.9 14.4 %copy-start.3 = (bf16[4,512,512]{2,1,0:T(8,128)(2,1)S(1)}, bf16[4,512,512]{2,1,0:T(8,128)(2,1)}, u32[]{:S(2)}) copy-start(bf16[4,512,512]{2,1,0:T(8,128)(2,1)} %copy.148) | copy-start | bytes 6291460
where the time goes:
time: 298 us; the launch traced here: 296 us
  starting transfers between devices  115 us (39%)
  blocking collectives  75.6 us (25%)
  local copies, waits for them, and re-layouts  40.9 us (14%)
  waiting for transfers between devices  31.1 us (10%)
  other arithmetic  19 us (6%)
  matrix products  14.5 us (5%)
    all_gather x2, blocking collectives, all_blocks(): tiles = lax.all_gather(tiles, axes[k], axis=0, tiled=True)  59.5 us
    ppermute x16, starting transfers between devices, shifted(): return lax.ppermute(value, axis, pairs)  49.4 us
    unnamed x53, local copies, waits for them, and re-layouts  27.3 us
    all_to_all x1, starting transfers between devices, body(): lax.all_to_all(to_slots(query_rows), SEQ, split_axis=0, concat_axis=0, ti...  18.5 us
    all_to_all x1, waiting for transfers between devices, body(): lax.all_to_all(to_slots(value_rows), SEQ, split_axis=0, concat_axis=0, ti...  18.4 us
    all_to_all x1, starting transfers between devices, exchange_in_order(): lax.all_to_all(tiles, axes[k], split_axis=k, concat_axis=k, tiled=True)  17.9 us
    all_to_all x1, starting transfers between devices, body(): lax.all_to_all(to_slots(value_rows), SEQ, split_axis=0, concat_axis=0, ti...  15.4 us
    all_gather x1, blocking collectives, body(): lax.all_gather(attended, 'head', axis=1, tiled=True)  11.7 us
  transfers between devices with their start and end apart: 21, of which 5 were waited for; matrix products, arithmetic and copies ran while one was open for 20% of the time, Pallas kernels for 0%

commit v1 on v0

v1 whole, which is shorter than its diff:
```python
import jax
import jax.numpy as jnp
from jax import lax
from jax.experimental import pallas as pl
from jax.experimental.pallas import tpu as pltpu
from jax.sharding import Mesh
from jax.sharding import PartitionSpec as P

HD = 128
BLOCK = 8
WINDOW = 1024
SEQ = ("seq_0", "seq_1", "seq_2")
MESH = pl.DeviceIdType.MESH
TILE = 128
PIECE = 4 * TILE
ID_ROWS = 16
ROWS = PIECE + 2 * ID_ROWS
SUBS = 2
SUB = ROWS // SUBS
STEPS = 5
NEG = -1e30
F32 = jnp.float32
BF16 = jnp.bfloat16


def kernel(
    q_in, k_in, v_in, w_in, id_in, out_ref,
    q_buf, slots, o_buf, att, w_buf, part, parts_in, m_r, m_l, acc_r, acc_l, q_id,
    u_send, u_recv, ag_send, ag_recv, ret_send, ret_recv, rs_send, rs_recv, w_sem,
):
    z, y, c = (lax.axis_index(a) for a in SEQ)
    x = lax.axis_index("head")
    nz, nx = lax.axis_size("seq_0"), lax.axis_size("head")
    par = y % 2
    mate = y + 1 - 2 * par
    twin = 1 - c
    piece = 4 * z + 2 * par + c
    place = 2 * par + c
    head = y // 2
    z_up, z_down = (z + 1) % nz, (z + nz - 1) % nz
    dests = [(2 * i + y // 4, (y % 4) // 2) for i in range(4)]
    sources = [(4 * par + 2 * c + r // 2, r % 2 + 0 * c) for r in range(4)]

    def other(yy, cc):
        return jnp.logical_or(yy != y, cc != c)

    def remote(src, dst, send_sem, recv_sem, to):
        return pltpu.make_async_remote_copy(
            src_ref=src, dst_ref=dst, send_sem=send_sem, recv_sem=recv_sem,
            device_id=to, device_id_type=MESH,
        )

    here = (z, mate, c, x)

    def wait_recv(dst, sem):
        remote(dst, dst, sem, sem, here).wait_recv()

    def wait_send(src, sem):
        remote(src, src, sem, sem, here).wait_send()

    w_copy = pltpu.make_async_copy(w_in, w_buf, w_sem)
    w_copy.start()

    barrier = pltpu.get_barrier_semaphore()
    apart = jnp.int32(0)
    for yy, cc in dests + sources:
        far = other(yy, cc)
        apart = apart + far.astype(jnp.int32)

        @pl.when(far)
        def _():
            pl.semaphore_signal(barrier, 1, device_id=(z, yy, cc, x), device_id_type=MESH)

    near = [(z_up, y, c, x), (z_down, y, c, x), (z, mate, c, x), (z, y, twin, x)]
    near += [(z, y, c, (x + d) % nx) for d in range(1, 4)]
    for to in near:
        pl.semaphore_signal(barrier, 1, device_id=to, device_id_type=MESH)
    pl.semaphore_wait(barrier, apart + len(near))

    def landing(j, r):
        rows = pl.ds(pl.multiple_of(r * TILE, TILE), TILE)
        ids = pl.ds(pl.multiple_of(PIECE + ID_ROWS * (r // 2), ID_ROWS), ID_ROWS)
        lanes = pl.ds(pl.multiple_of(HD * (r % 2), HD), HD)
        return [
            slots.at[j, rows, 0:HD],
            slots.at[j, rows, HD : 2 * HD],
            slots.at[j, ids, lanes],
            q_buf.at[rows, :],
        ]

    for i, (yy, cc) in enumerate(dests):
        lanes = slice(i * HD, (i + 1) * HD)
        leaving = [k_in.at[:, lanes], v_in.at[:, lanes], id_in, q_in.at[:, lanes]]
        landed = landing(4 * z + 2 * (yy % 2) + cc, place)
        far = other(yy, cc)

        @pl.when(far)
        def _():
            for t in range(4):
                remote(
                    leaving[t], landed[t], u_send.at[i, t], u_recv.at[place, t], (z, yy, cc, x)
                ).start()

        @pl.when(jnp.logical_not(far))
        def _():
            for t in range(4):
                pltpu.make_async_copy(leaving[t], landed[t], u_recv.at[place, t]).start()

    m_r[...] = jnp.full_like(m_r, NEG)
    m_l[...] = jnp.full_like(m_l, NEG)
    acc_r[...] = jnp.zeros_like(acc_r)
    acc_l[...] = jnp.zeros_like(acc_l)

    def step_of(s, d):
        down = jnp.where(s <= 4, -s, -3), (s == 5)
        up = jnp.where(s <= 3, s, s - 3), (s >= 4)
        across = jnp.where(s <= 3, 1 - s, s - 1), (s >= 1)
        dz = jnp.where(d == 0, down[0], jnp.where(d == 1, up[0], across[0]))
        flip = jnp.where(d == 0, down[1], jnp.where(d == 1, up[1], across[1]))
        return dz, flip.astype(jnp.int32)

    def slot_of(dz, flip):
        return 4 * ((z + dz + nz) % nz) + 2 * (par + flip - 2 * par * flip) + c

    def sub_of(j, sub):
        return slots.at[j, pl.ds(sub * SUB, SUB), :]

    targets = [(z_up, y, c, x), (z_down, y, c, x), (z, mate, c, x)]

    def send_step(s, sub):
        for d, (shift, turn) in enumerate(((1, 0), (-1, 0), (0, 1))):
            dz, flip = step_of(s, d)
            j = slot_of(dz + shift, jnp.int32(0) if turn else flip)
            ref = sub_of(j, sub)
            remote(ref, ref, ag_send.at[d, s, sub], ag_recv.at[j, sub], targets[d]).start()

    def send_twin(j, d, s, sub):
        ref = sub_of(j, sub)
        remote(ref, ref, ag_send.at[3 + d, s, sub], ag_recv.at[j, sub], (z, y, twin, x)).start()

    for r in range(4):
        landed = landing(piece, r)
        for t in range(3):
            wait_recv(landed[t], u_recv.at[r, t])
    for sub in range(SUBS):
        send_step(jnp.int32(1), sub)
        send_twin(piece, 0, 0, sub)
    for r in range(4):
        wait_recv(landing(piece, r)[3], u_recv.at[r, 3])

    def ids_of(j):
        first = slots[j, PIECE : PIECE + ID_ROWS, :].astype(F32)[0:1, :]
        second = slots[j, PIECE + ID_ROWS : ROWS, :].astype(F32)[0:1, :]
        return jnp.concatenate([first, second], axis=1)

    own_ids = ids_of(piece)
    eye = lax.broadcasted_iota(jnp.int32, (TILE, TILE), 0) == lax.broadcasted_iota(
        jnp.int32, (TILE, TILE), 1
    )
    for r in range(4):
        row = jnp.broadcast_to(own_ids[:, r * TILE : (r + 1) * TILE], (TILE, TILE))
        column = jnp.sum(jnp.where(eye, row, 0.0), axis=1, keepdims=True)
        q_id[r * TILE : (r + 1) * TILE, :] = jnp.broadcast_to(column, (TILE, TILE))

    factor = HD ** -0.5 * 1.4426950408889634

    def across_keys(col):
        return jnp.concatenate([col] * 4, axis=1)

    def accumulate(scores, values, rows, m_ref, acc_ref):
        before = m_ref[rows, :]
        after = jnp.maximum(before, jnp.max(scores, axis=1, keepdims=True))
        weights = jnp.exp2(scores - across_keys(after))
        kept = jnp.exp2(before - after)
        m_ref[rows, :] = after
        acc_ref[rows, :] = acc_ref[rows, :] * jnp.concatenate([kept, kept], axis=1) + jnp.dot(
            weights.astype(BF16), values, preferred_element_type=F32
        )

    def attend(j, near_by):
        keys = slots[j, 0:PIECE, 0:HD]
        values = jnp.concatenate(
            [slots[j, 0:PIECE, HD : 2 * HD], jnp.ones((PIECE, HD), BF16)], axis=1
        )
        key_ids = ids_of(j)
        for r in range(4):
            rows = slice(r * TILE, (r + 1) * TILE)
            scores = lax.dot_general(
                q_buf[rows, :], keys, (((1,), (1,)), ((), ())), preferred_element_type=F32
            ) * factor
            same = across_keys(q_id[rows, :]) == key_ids
            if near_by:
                ahead = (
                    (j - piece) * PIECE - r * TILE
                    + lax.broadcasted_iota(jnp.int32, (TILE, PIECE), 1)
                    - lax.broadcasted_iota(jnp.int32, (TILE, PIECE), 0)
                )
                causal = ahead <= 0
                same = jnp.logical_and(same, causal)
                window = jnp.logical_and(causal, ahead > -WINDOW)
                accumulate(jnp.where(window, scores, NEG), values, rows, m_l, acc_l)
            accumulate(jnp.where(same, scores, NEG), values, rows, m_r, acc_r)

    def turn(t, carry):
        s = jnp.where(t < 2, 0, (t - 2) // 6 + 1)
        d6 = jnp.where(t < 2, 3 * t, (t - 2) % 6)
        d = d6 % 3
        from_twin = d6 // 3

        @pl.when(jnp.logical_and(t >= 2, d6 == 0))
        def _():
            for sub in range(SUBS):
                arrived = [slot_of(*step_of(s, e)) for e in range(3)]
                for e in range(3):
                    wait_recv(sub_of(arrived[e], sub), ag_recv.at[arrived[e], sub])

                @pl.when(s < STEPS)
                def _():
                    send_step(s + 1, sub)

                for e in range(3):
                    send_twin(arrived[e], e, s, sub)

        dz, flip = step_of(s, d)
        first = (s > 0).astype(jnp.int32)
        j = slot_of(dz * first, flip * first)
        j = j + from_twin * (1 - 2 * c)

        @pl.when(from_twin == 1)
        def _():
            for sub in range(SUBS):
                wait_recv(sub_of(j, sub), ag_recv.at[j, sub])

        back = piece - j

        @pl.when(jnp.logical_and(back >= 0, back <= 2))
        def _():
            attend(j, True)

        @pl.when(back > 2)
        def _():
            attend(j, False)

        return carry

    lax.fori_loop(0, 2 + 6 * STEPS, turn, 0)

    columns = pl.ds(pl.multiple_of(head * HD, HD), HD)
    for r, (yy, cc) in enumerate(sources):
        rows = slice(r * TILE, (r + 1) * TILE)
        routed = (acc_r[rows, 0:HD] / acc_r[rows, HD : 2 * HD]).astype(BF16).astype(F32)
        local = acc_l[rows, 0:HD] / acc_l[rows, HD : 2 * HD]
        o_buf[rows, :] = (routed + local).astype(BF16)
        far = other(yy, cc)

        @pl.when(far)
        def _():
            remote(
                o_buf.at[rows, :], att.at[:, columns], ret_send.at[r], ret_recv.at[head],
                (z, yy, cc, x),
            ).start()

        @pl.when(jnp.logical_not(far))
        def _():
            pltpu.make_async_copy(o_buf.at[rows, :], att.at[:, columns], ret_recv.at[head]).start()

    w_copy.wait()
    for i in range(4):
        wait_recv(att.at[:, i * HD : (i + 1) * HD], ret_recv.at[i])

    def partial(column_of):
        columns = pl.ds(pl.multiple_of(column_of * 4 * HD, 4 * HD), 4 * HD)
        return jnp.dot(att[...], w_buf[:, columns], preferred_element_type=F32)

    for d in (2, 1, 3):
        to = (x + d) % nx
        part[d - 1] = partial(to).astype(BF16)
        remote(
            part.at[d - 1], parts_in.at[d - 1], rs_send.at[d - 1], rs_recv.at[d - 1], (z, y, c, to)
        ).start()
    total = partial(x)
    for d in (1, 3, 2):
        wait_recv(parts_in.at[d - 1], rs_recv.at[d - 1])
        total = total + parts_in[d - 1].astype(F32)
    out_ref[...] = total.astype(BF16)

    for i, (yy, cc) in enumerate(dests):
        lanes = slice(i * HD, (i + 1) * HD)

        @pl.when(other(yy, cc))
        def _():
            for t, ref in enumerate((k_in.at[:, lanes], v_in.at[:, lanes], id_in, q_in.at[:, lanes])):
                wait_send(ref, u_send.at[i, t])

    for r, (yy, cc) in enumerate(sources):
        @pl.when(other(yy, cc))
        def _():
            wait_send(o_buf.at[r * TILE : (r + 1) * TILE, :], ret_send.at[r])

    for sub in range(SUBS):
        wait_send(sub_of(0, sub), ag_send.at[3, 0, sub])

    def settle(s, carry):
        for d in range(6):
            for sub in range(SUBS):
                wait_send(sub_of(0, sub), ag_send.at[d, s, sub])
        return carry

    lax.fori_loop(1, STEPS + 1, settle, 0)
    for d in range(3):
        wait_send(part.at[d], rs_send.at[d])


def body(query_rows, key_rows, value_rows, out_weight, cluster_ids):
    tokens, width = query_rows.shape
    ids = jnp.repeat(cluster_ids[0], BLOCK).astype(BF16)
    ids = jnp.broadcast_to(ids[None, :], (ID_ROWS, tokens))
    dma = pltpu.SemaphoreType.DMA
    return pl.pallas_call(
        kernel,
        out_shape=jax.ShapeDtypeStruct((tokens, width), BF16),
        in_specs=[pl.BlockSpec(memory_space=pl.ANY)] * 5,
        out_specs=pl.BlockSpec(memory_space=pltpu.VMEM),
        scratch_shapes=[
            pltpu.VMEM((PIECE, HD), BF16),
            pltpu.VMEM((32, ROWS, 2 * HD), BF16),
            pltpu.VMEM((PIECE, HD), BF16),
            pltpu.VMEM((tokens, width), BF16),
            pltpu.VMEM(out_weight.shape, BF16),
            pltpu.VMEM((3, tokens, width), BF16),
            pltpu.VMEM((3, tokens, width), BF16),
            pltpu.VMEM((PIECE, HD), F32),
            pltpu.VMEM((PIECE, HD), F32),
            pltpu.VMEM((PIECE, 2 * HD), F32),
            pltpu.VMEM((PIECE, 2 * HD), F32),
            pltpu.VMEM((PIECE, HD), F32),
            dma((4, 4)),
            dma((4, 4)),
            dma((6, STEPS + 1, SUBS)),
            dma((32, SUBS)),
            dma((4,)),
            dma((4,)),
            dma((3,)),
            dma((3,)),
            dma,
        ],
        compiler_params=pltpu.CompilerParams(collective_id=0, has_side_effects=True),
        name="attention",
    )(query_rows, key_rows, value_rows, out_weight, ids)


def solution(mesh):
    split = Mesh(
        mesh.devices.reshape(8, 8, 2, mesh.shape["head"]), ("seq_0", "seq_1", "seq_2", "head")
    )
    return jax.shard_map(
        body,
        mesh=split,
        in_specs=(P(SEQ, "head"), P(SEQ, "head"), P(SEQ, "head"), P("head", None), P(SEQ, None)),
        out_specs=P(SEQ, "head"),
        check_vma=False,
    )
```

time: 298 us -> 84.4 us (0.28)
  starting transfers between devices: 115 us -> 0 us
  Pallas kernels: 0 us -> 81.2 us
  blocking collectives: 75.6 us -> 0 us
  local copies, waits for them, and re-layouts: 40.9 us -> 2.34 us
  waiting for transfers between devices: 31.1 us -> 0 us
  other arithmetic: 19 us -> 0.66 us
  matrix products: 14.5 us -> 0 us
    pallas_call x0 -> x1, Pallas kernels: none -> 81.2 us  [body(): pl.pallas_call(kernel, out_shape=jax.ShapeDtypeStruct((tokens, width), BF...]
    all_gather x3 -> x0, blocking collectives: 71.2 us -> none  [the longest x2 59.5 us: all_blocks(): tiles = lax.all_gather(tiles, axes[k], axis=0, tiled=True)]
    all_to_all x5 -> x0, starting transfers between devices: 65.4 us -> none  [the longest x1 18.5 us: body(): lax.all_to_all(to_slots(query_rows), SEQ, split_axis=0, concat_axis=0, ti...]
    ppermute x16 -> x0, starting transfers between devices: 49.4 us -> none  [shifted(): return lax.ppermute(value, axis, pairs)]
    unnamed x53 -> x1, local copies, waits for them, and re-layouts: 27.3 us -> 1.57 us
    all_to_all x5 -> x0, waiting for transfers between devices: 20.2 us -> none  [the longest x1 18.4 us: body(): lax.all_to_all(to_slots(value_rows), SEQ, split_axis=0, concat_axis=0, ti...]
    ppermute x16 -> x0, waiting for transfers between devices: 10.8 us -> none  [shifted(): return lax.ppermute(value, axis, pairs)]
    dot_general x6 -> x0, matrix products: 10.6 us -> none  [the longest x3 7.45 us: attend(): jnp.einsum('hqk,khd->qhd', weights, values_h, preferred_element_type=jnp....]
  transfers between devices with their start and end apart: 21 -> 0, of which waited for: 5 -> 0; matrix products, arithmetic and copies ran while one was open for 20% -> 0% of each run, Pallas kernels for 0% -> 0%
where the time goes in v1:
time: 84.4 us; the launch traced here: 84.2 us
  Pallas kernels  81.2 us (96%)
  local copies, waits for them, and re-layouts  2.34 us (3%)
    pallas_call x1, Pallas kernels, body(): pl.pallas_call(kernel, out_shape=jax.ShapeDtypeStruct((tokens, width), BF...  81.2 us

profile of v1, /device:TPU:1, one launch (start us, length us, event | category | flops | bytes accessed | tf_op | source)
XLA Modules:
  0.0 84.2 jit_solution(14122362395725503781)
XLA Ops:
  0.0 0.7 convert_bitcast_fusion
  0.7 0.1 broadcast_in_dim.4
  0.7 0.1 convert_element_type.16
  0.8 0.6 broadcast_in_dim.10.id_in
  1.4 81.2 %attention.1 = bf16[128,512]{1,0:T(8,128)(2,1)} custom-call(bf16[128,512]{1,0:T(8,128)(2,1)} %q_in.1, bf16[128,512]{1,0:T(8,128)(2,1)} %k_in.1, bf16[128,512]{1,0:T(8,128)(2,1)} %v_in.1, bf16[512,2048]{1,0:T(8,128)(2,1)} %w_in.1, bf16[16,128]{1,0:T(8,128)(2,1)} %broadcast_in_dim.10.id_in), custom_call_target="tpu_custom_call" | custom-call | tf_op jit(solution)/shard_map/attention/pallas_call | solution.py:319
  82.6 1.6 %copy.7 = bf16[128,512]{1,0:T(8,128)(2,1)} copy(bf16[128,512]{1,0:T(8,128)(2,1)} %attention.1) | data formatting | bytes 262144

commit v2 on v1

v2 whole, which is shorter than its diff:
```python
import jax
import jax.numpy as jnp
from jax import lax
from jax.experimental import pallas as pl
from jax.experimental.pallas import tpu as pltpu
from jax.sharding import Mesh
from jax.sharding import PartitionSpec as P

HD = 128
BLOCK = 8
WINDOW = 1024
SEQ = ("seq_0", "seq_1", "seq_2")
MESH = pl.DeviceIdType.MESH
TILE = 128
PIECE = 4 * TILE
SUBS = 4
STEPS = 5
NEG = -1e30
F32 = jnp.float32
BF16 = jnp.bfloat16


def kernel(
    q_in, k_in, v_in, w_in, id_in, out_ref,
    q_buf, slots, id_row, id_slots, o_buf, att, w_buf, part, relay_out, relay_in, parts_in,
    m_r, m_l, acc_r, acc_l, q_id,
    u_send, u_recv, ag_send, ag_recv, id_send, id_recv, ret_send, ret_recv, rs_send, rs_recv, w_sem,
):
    z, y, c = (lax.axis_index(a) for a in SEQ)
    x = lax.axis_index("head")
    nz, ny, nx = lax.axis_size("seq_0"), lax.axis_size("seq_1"), lax.axis_size("head")
    par = y % 2
    mate = y + 1 - 2 * par
    twin = 1 - c
    piece = 4 * z + 2 * c + par
    place = 2 * ((y // 2) % 2) + c
    head = y // 2
    z_up, z_down = (z + 1) % nz, (z + nz - 1) % nz
    x_up, x_down = (x + 1) % nx, (x + nx - 1) % nx
    dests = [(y + far) % ny for far in (3, ny - 3, 1, ny - 1)]
    sources = [(1 - par + 4 * c + 2 * (r // 2), r % 2) for r in range(4)]

    def remote(src, dst, send_sem, recv_sem, to):
        return pltpu.make_async_remote_copy(
            src_ref=src, dst_ref=dst, send_sem=send_sem, recv_sem=recv_sem,
            device_id=to, device_id_type=MESH,
        )

    here = (z, mate, c, x)

    def wait_recv(dst, sem):
        remote(dst, dst, sem, sem, here).wait_recv()

    def wait_send(src, sem):
        remote(src, src, sem, sem, here).wait_send()

    barrier = pltpu.get_barrier_semaphore()
    near = [(z, yy, y // 4, x) for yy in dests] + [(z, yy, cc, x) for yy, cc in sources]
    near += [(z_up, y, c, x), (z_down, y, c, x), (z, mate, c, x), (z, y, twin, x)]
    near += [(z, y, c, x_up), (z, y, c, x_down)]
    for to in near:
        pl.semaphore_signal(barrier, 1, device_id=to, device_id_type=MESH)

    w_copy = pltpu.make_async_copy(w_in, w_buf, w_sem)
    w_copy.start()
    block_of = lax.broadcasted_iota(jnp.int32, (1, TILE), 1) // BLOCK
    row = jnp.zeros((1, TILE), jnp.int32)
    for b in range(TILE // BLOCK):
        row = jnp.where(block_of == b, id_in[0, b], row)
    id_row[...] = row
    m_r[...] = jnp.full_like(m_r, NEG)
    m_l[...] = jnp.full_like(m_l, NEG)
    acc_r[...] = jnp.zeros_like(acc_r)
    acc_l[...] = jnp.zeros_like(acc_l)

    pl.semaphore_wait(barrier, len(near))

    def rows_of(r):
        return pl.ds(pl.multiple_of(r * TILE, TILE), TILE)

    def landing(j, r):
        return [
            slots.at[j, rows_of(r), 0:HD],
            slots.at[j, rows_of(r), HD : 2 * HD],
            id_slots.at[j, r],
            q_buf.at[rows_of(r), :],
        ]

    def leaving(yy):
        lanes = pl.ds(pl.multiple_of((yy // 2) * HD, HD), HD)
        return [k_in.at[:, lanes], v_in.at[:, lanes], id_row, q_in.at[:, lanes]]

    for tensors in ((0, 1, 2), (3,)):
        for i, yy in enumerate(dests):
            landed = landing(4 * z + 2 * (y // 4) + (1 - par), place)
            for t in tensors:
                remote(
                    leaving(yy)[t], landed[t], u_send.at[i, t], u_recv.at[place, t],
                    (z, yy, y // 4, x),
                ).start()

    def step_of(s, d):
        down = jnp.where(s <= 4, -s, -3), (s == 5)
        up = jnp.where(s <= 3, s, s - 3), (s >= 4)
        across = jnp.where(s <= 3, 1 - s, s - 1), (s >= 1)
        dz = jnp.where(d == 0, down[0], jnp.where(d == 1, up[0], across[0]))
        flip = jnp.where(d == 0, down[1], jnp.where(d == 1, up[1], across[1]))
        return dz, flip.astype(jnp.int32)

    def slot_of(dz, flip):
        return 4 * ((z + dz + nz) % nz) + 2 * c + par + flip - 2 * par * flip

    def sub_of(j, sub):
        return slots.at[j, rows_of(sub), :]

    targets = [(z_up, y, c, x), (z_down, y, c, x), (z, mate, c, x)]

    def send(j, d, s, sub, to):
        ref = sub_of(j, sub)
        remote(ref, ref, ag_send.at[d, s, sub], ag_recv.at[j, sub], to).start()

    def send_ids(j, d, s, to):
        remote(id_slots.at[j], id_slots.at[j], id_send.at[d, s], id_recv.at[j], to).start()

    def source_slots(s):
        found = []
        for d, (shift, turned) in enumerate(((1, 0), (-1, 0), (0, 1))):
            dz, flip = step_of(s, d)
            found.append(slot_of(dz + shift, jnp.int32(0) if turned else flip))
        return found

    for r in range(4):
        landed = landing(piece, r)
        for t in range(3):
            wait_recv(landed[t], u_recv.at[r, t])
        for d in range(3):
            send(piece, d, 1, r, targets[d])
        send(piece, 3, 0, r, (z, y, twin, x))
    for d in range(3):
        send_ids(piece, d, 1, targets[d])
    send_ids(piece, 3, 0, (z, y, twin, x))

    def ids_of(j):
        return jnp.concatenate([id_slots[j, r] for r in range(4)], axis=1).astype(F32)

    own_ids = ids_of(piece)
    eye = lax.broadcasted_iota(jnp.int32, (TILE, TILE), 0) == lax.broadcasted_iota(
        jnp.int32, (TILE, TILE), 1
    )
    for r in range(4):
        row = jnp.broadcast_to(own_ids[:, r * TILE : (r + 1) * TILE], (TILE, TILE))
        column = jnp.sum(jnp.where(eye, row, 0.0), axis=1, keepdims=True)
        q_id[r * TILE : (r + 1) * TILE, :] = jnp.broadcast_to(column, (TILE, TILE))
    for r in range(4):
        wait_recv(landing(piece, r)[3], u_recv.at[r, 3])

    factor = HD ** -0.5 * 1.4426950408889634

    def across_keys(col):
        return jnp.concatenate([col] * 4, axis=1)

    def accumulate(scores, values, rows, m_ref, acc_ref):
        before = m_ref[rows, :]
        after = jnp.maximum(before, jnp.max(scores, axis=1, keepdims=True))
        weights = jnp.exp2(scores - across_keys(after))
        kept = jnp.exp2(before - after)
        m_ref[rows, :] = after
        acc_ref[rows, :] = acc_ref[rows, :] * jnp.concatenate([kept, kept], axis=1) + jnp.dot(
            weights.astype(BF16), values, preferred_element_type=F32
        )

    def start_of(j):
        return 1024 * (j // 2) + 256 * (1 - j % 2)

    def attend(j, near_by):
        keys = slots[j, :, 0:HD]
        values = jnp.concatenate([slots[j, :, HD : 2 * HD], jnp.ones((PIECE, HD), BF16)], axis=1)
        key_ids = ids_of(j)
        for r in range(4):
            rows = slice(r * TILE, (r + 1) * TILE)
            scores = lax.dot_general(
                q_buf[rows, :], keys, (((1,), (1,)), ((), ())), preferred_element_type=F32
            ) * factor
            same = across_keys(q_id[rows, :]) == key_ids
            if near_by:
                lane = lax.broadcasted_iota(jnp.int32, (TILE, PIECE), 1)
                ahead = (
                    start_of(j) - start_of(piece) - r * TILE - 256 * (r // 2)
                    + lane + jnp.where(lane >= 256, 256, 0)
                    - lax.broadcasted_iota(jnp.int32, (TILE, PIECE), 0)
                )
                causal = ahead <= 0
                same = jnp.logical_and(same, causal)
                window = jnp.logical_and(causal, ahead > -WINDOW)
                accumulate(jnp.where(window, scores, NEG), values, rows, m_l, acc_l)
            accumulate(jnp.where(same, scores, NEG), values, rows, m_r, acc_r)

    def turn(t, carry):
        s, k = t // 6, t % 6
        d, from_twin = k % 3, k // 3
        dz, flip = step_of(s, d)
        later = (s > 0).astype(jnp.int32)
        j = slot_of(dz * later, flip * later) + from_twin * (2 - 4 * c)
        used = jnp.logical_or(s > 0, d == 0)

        @pl.when(jnp.logical_and(used, from_twin == 1))
        def _():
            wait_recv(id_slots.at[j], id_recv.at[j])
            for sub in range(SUBS):
                wait_recv(sub_of(j, sub), ag_recv.at[j, sub])

        back = piece // 2 - j // 2

        @pl.when(jnp.logical_and(used, jnp.logical_and(back >= 0, back <= 1)))
        def _():
            attend(j, True)

        @pl.when(jnp.logical_and(used, back > 1))
        def _():
            attend(j, False)

        @pl.when(jnp.logical_and(s < STEPS, d != 1))
        def _():
            sub = (2 * k) // 3
            arrived = [slot_of(*step_of(s + 1, e)) for e in range(3)]
            onward = source_slots(s + 2)
            for e in range(3):
                wait_recv(sub_of(arrived[e], sub), ag_recv.at[arrived[e], sub])

            @pl.when(s + 1 < STEPS)
            def _():
                for e in range(3):
                    send(onward[e], e, s + 2, sub, targets[e])

            for e in range(3):
                send(arrived[e], 3 + e, s + 1, sub, (z, y, twin, x))

            @pl.when(sub == 0)
            def _():
                for e in range(3):
                    wait_recv(id_slots.at[arrived[e]], id_recv.at[arrived[e]])

                @pl.when(s + 1 < STEPS)
                def _():
                    for e in range(3):
                        send_ids(onward[e], e, s + 2, targets[e])

                for e in range(3):
                    send_ids(arrived[e], 3 + e, s + 1, (z, y, twin, x))

        return carry

    lax.fori_loop(0, 6 * (STEPS + 1), turn, 0)

    columns = pl.ds(pl.multiple_of(head * HD, HD), HD)
    for r, (yy, cc) in enumerate(sources):
        rows = slice(r * TILE, (r + 1) * TILE)
        routed = (acc_r[rows, 0:HD] / acc_r[rows, HD : 2 * HD]).astype(BF16).astype(F32)
        local = acc_l[rows, 0:HD] / acc_l[rows, HD : 2 * HD]
        o_buf[rows, :] = (routed + local).astype(BF16)
        remote(
            o_buf.at[rows, :], att.at[:, columns], ret_send.at[r], ret_recv.at[head],
            (z, yy, cc, x),
        ).start()

    w_copy.wait()
    for i in range(4):
        wait_recv(att.at[:, i * HD : (i + 1) * HD], ret_recv.at[i])

    def partial(column_of):
        columns = pl.ds(pl.multiple_of(column_of * 4 * HD, 4 * HD), 4 * HD)
        return jnp.dot(att[...], w_buf[:, columns], preferred_element_type=F32)

    low, high = slice(0, TILE // 2), slice(TILE // 2, TILE)
    sides = ((x_up, low, high), (x_down, high, low))
    part[2] = partial((x + 2) % nx).astype(BF16)
    for e, (to, passed, _) in enumerate(sides):
        remote(
            part.at[2, passed, :], relay_in.at[e], rs_send.at[e, 0], rs_recv.at[e, 0], (z, y, c, to)
        ).start()
    sums = []
    for e, (to, passed, direct) in enumerate(sides):
        here_sum = partial(to)
        part[e] = here_sum.astype(BF16)
        remote(
            part.at[e, direct, :], parts_in.at[e, direct, :], rs_send.at[e, 1], rs_recv.at[e, 1],
            (z, y, c, to),
        ).start()
        sums.append(here_sum[passed, :])
    total = partial(x)
    for e, (to, passed, direct) in enumerate(sides):
        wait_recv(relay_in.at[e], rs_recv.at[e, 0])
        relay_out[e] = (sums[e] + relay_in[e].astype(F32)).astype(BF16)
        remote(
            relay_out.at[e], parts_in.at[e, passed, :], rs_send.at[e, 2], rs_recv.at[e, 2],
            (z, y, c, to),
        ).start()
    for e, (to, passed, direct) in enumerate(sides):
        wait_recv(parts_in.at[e, direct, :], rs_recv.at[e, 1])
    for e, (to, passed, direct) in enumerate(sides):
        wait_recv(parts_in.at[e, passed, :], rs_recv.at[e, 2])
    out_ref[...] = (total + parts_in[0].astype(F32) + parts_in[1].astype(F32)).astype(BF16)

    for i, yy in enumerate(dests):
        for t, ref in enumerate(leaving(yy)):
            wait_send(ref, u_send.at[i, t])
    for r in range(4):
        wait_send(o_buf.at[r * TILE : (r + 1) * TILE, :], ret_send.at[r])
    wait_send(id_slots.at[0], id_send.at[3, 0])
    for sub in range(SUBS):
        wait_send(sub_of(0, sub), ag_send.at[3, 0, sub])

    def settle(s, carry):
        for d in range(6):
            wait_send(id_slots.at[0], id_send.at[d, s])
            for sub in range(SUBS):
                wait_send(sub_of(0, sub), ag_send.at[d, s, sub])
        return carry

    lax.fori_loop(1, STEPS + 1, settle, 0)
    for e in range(2):
        for n in range(3):
            wait_send(relay_out.at[e], rs_send.at[e, n])


def body(query_rows, key_rows, value_rows, out_weight, cluster_ids):
    tokens, width = query_rows.shape
    dma = pltpu.SemaphoreType.DMA
    anywhere = pl.BlockSpec(memory_space=pl.ANY)
    return pl.pallas_call(
        kernel,
        out_shape=jax.ShapeDtypeStruct((tokens, width), BF16),
        in_specs=[anywhere] * 4 + [pl.BlockSpec(memory_space=pltpu.SMEM)],
        out_specs=pl.BlockSpec(memory_space=pltpu.VMEM),
        scratch_shapes=[
            pltpu.VMEM((PIECE, HD), BF16),
            pltpu.VMEM((32, PIECE, 2 * HD), BF16),
            pltpu.VMEM((1, TILE), jnp.int32),
            pltpu.VMEM((32, 4, 1, TILE), jnp.int32),
            pltpu.VMEM((PIECE, HD), BF16),
            pltpu.VMEM((tokens, width), BF16),
            pltpu.VMEM(out_weight.shape, BF16),
            pltpu.VMEM((3, tokens, width), BF16),
            pltpu.VMEM((2, tokens // 2, width), BF16),
            pltpu.VMEM((2, tokens // 2, width), BF16),
            pltpu.VMEM((2, tokens, width), BF16),
            pltpu.VMEM((PIECE, HD), F32),
            pltpu.VMEM((PIECE, HD), F32),
            pltpu.VMEM((PIECE, 2 * HD), F32),
            pltpu.VMEM((PIECE, 2 * HD), F32),
            pltpu.VMEM((PIECE, HD), F32),
            dma((4, 4)),
            dma((4, 4)),
            dma((6, STEPS + 1, SUBS)),
            dma((32, SUBS)),
            dma((6, STEPS + 1)),
            dma((32,)),
            dma((4,)),
            dma((4,)),
            dma((2, 3)),
            dma((2, 3)),
            dma,
        ],
        compiler_params=pltpu.CompilerParams(collective_id=0, has_side_effects=True),
        name="attention",
    )(query_rows, key_rows, value_rows, out_weight, cluster_ids)


def solution(mesh):
    split = Mesh(
        mesh.devices.reshape(8, 8, 2, mesh.shape["head"]), ("seq_0", "seq_1", "seq_2", "head")
    )
    return jax.shard_map(
        body,
        mesh=split,
        in_specs=(P(SEQ, "head"), P(SEQ, "head"), P(SEQ, "head"), P("head", None), P(SEQ, None)),
        out_specs=P(SEQ, "head"),
        check_vma=False,
    )
```

time: 84.4 us -> 75.1 us (0.89)
  Pallas kernels: 81.2 us -> 73.1 us
    pallas_call x1, Pallas kernels: 81.2 us -> 73.1 us  [body(): pl.pallas_call(kernel, out_shape=jax.ShapeDtypeStruct((tokens, width), BF...]
where the time goes in v2:
time: 75.1 us; the launch traced here: 74.7 us
  Pallas kernels  73.1 us (97%)
  local copies, waits for them, and re-layouts  1.57 us (2%)
    pallas_call x1, Pallas kernels, body(): pl.pallas_call(kernel, out_shape=jax.ShapeDtypeStruct((tokens, width), BF...  73.1 us
    unnamed x1, local copies, waits for them, and re-layouts  1.57 us

profile of v2, /device:TPU:1, one launch (start us, length us, event | category | flops | bytes accessed | tf_op | source)
XLA Modules:
  0.0 74.7 jit_solution(14631047735772589585)
XLA Ops:
  0.0 73.1 %attention.1 = bf16[128,512]{1,0:T(8,128)(2,1)} custom-call(bf16[128,512]{1,0:T(8,128)(2,1)} %q_in.1, bf16[128,512]{1,0:T(8,128)(2,1)} %k_in.1, bf16[128,512]{1,0:T(8,128)(2,1)} %v_in.1, bf16[512,2048]{1,0:T(8,128)(2,1)} %w_in.1, s32[1,16]{1,0:T(1,128)} %id_in.1), custom_call_target="tpu_custom_call" | custom-call | tf_op jit(solution)/shard_map/attention/pallas_call | solution.py:330
  73.1 1.6 %copy.7 = bf16[128,512]{1,0:T(8,128)(2,1)} copy(bf16[128,512]{1,0:T(8,128)(2,1)} %attention.1) | data formatting | bytes 262144

commit v3 on v2

--- a/solution.py
+++ b/solution.py
@@ -14,7 +14,7 @@
 TILE = 128
 PIECE = 4 * TILE
 SUBS = 4
-STEPS = 5
+STEPS = 4
 NEG = -1e30
 F32 = jnp.float32
 BF16 = jnp.bfloat16
@@ -22,9 +22,10 @@
 
 def kernel(
     q_in, k_in, v_in, w_in, id_in, out_ref,
-    q_buf, slots, id_row, id_slots, o_buf, att, w_buf, part, relay_out, relay_in, parts_in,
-    m_r, m_l, acc_r, acc_l, q_id,
-    u_send, u_recv, ag_send, ag_recv, id_send, id_recv, ret_send, ret_recv, rs_send, rs_recv, w_sem,
+    q_buf, slots, id_row, id_slots, o_buf, o_away, o_in, stats, stats_in, att, w_buf,
+    part, relay_out, relay_in, parts_in, m_r, m_l, acc_r, acc_l, q_id,
+    u_send, u_recv, ag_send, ag_recv, id_send, id_recv, y_send, q_recv, o_send, o_recv,
+    ret_send, ret_recv, rs_send, rs_recv, w_sem,
 ):
     z, y, c = (lax.axis_index(a) for a in SEQ)
     x = lax.axis_index("head")
@@ -99,60 +100,72 @@
                     (z, yy, y // 4, x),
                 ).start()
 
-    def step_of(s, d):
-        down = jnp.where(s <= 4, -s, -3), (s == 5)
-        up = jnp.where(s <= 3, s, s - 3), (s >= 4)
-        across = jnp.where(s <= 3, 1 - s, s - 1), (s >= 1)
-        dz = jnp.where(d == 0, down[0], jnp.where(d == 1, up[0], across[0]))
-        flip = jnp.where(d == 0, down[1], jnp.where(d == 1, up[1], across[1]))
-        return dz, flip.astype(jnp.int32)
-
-    def slot_of(dz, flip):
-        return 4 * ((z + dz + nz) % nz) + 2 * c + par + flip - 2 * par * flip
+    def slot_of(dz, core, p):
+        return 4 * ((z + dz + nz) % nz) + 2 * core + p
 
     def sub_of(j, sub):
         return slots.at[j, rows_of(sub), :]
 
-    targets = [(z_up, y, c, x), (z_down, y, c, x), (z, mate, c, x)]
-
-    def send(j, d, s, sub, to):
+    to_up, to_down, to_mate, to_twin = (z_up, y, c, x), (z_down, y, c, x), here, (z, y, twin, x)
+
+    def send(j, sub, send_sem, to):
         ref = sub_of(j, sub)
-        remote(ref, ref, ag_send.at[d, s, sub], ag_recv.at[j, sub], to).start()
-
-    def send_ids(j, d, s, to):
-        remote(id_slots.at[j], id_slots.at[j], id_send.at[d, s], id_recv.at[j], to).start()
-
-    def source_slots(s):
-        found = []
-        for d, (shift, turned) in enumerate(((1, 0), (-1, 0), (0, 1))):
-            dz, flip = step_of(s, d)
-            found.append(slot_of(dz + shift, jnp.int32(0) if turned else flip))
-        return found
+        remote(ref, ref, send_sem, ag_recv.at[j, sub], to).start()
+
+    def send_ids(j, send_sem, to):
+        remote(id_slots.at[j], id_slots.at[j], send_sem, id_recv.at[j], to).start()
+
+    def send_whole(j, n, to):
+        send_ids(j, y_send.at[n, SUBS], to)
+        for sub in range(SUBS):
+            send(j, sub, y_send.at[n, sub], to)
+
+    def wait_whole(j):
+        wait_recv(id_slots.at[j], id_recv.at[j])
+        for sub in range(SUBS):
+            wait_recv(sub_of(j, sub), ag_recv.at[j, sub])
 
     for r in range(4):
         landed = landing(piece, r)
         for t in range(3):
             wait_recv(landed[t], u_recv.at[r, t])
-        for d in range(3):
-            send(piece, d, 1, r, targets[d])
-        send(piece, 3, 0, r, (z, y, twin, x))
-    for d in range(3):
-        send_ids(piece, d, 1, targets[d])
-    send_ids(piece, 3, 0, (z, y, twin, x))
+        send(piece, r, ag_send.at[0, 1, r], to_up)
+        send(piece, r, ag_send.at[1, 1, r], to_down)
+        send(piece, r, ag_send.at[2, 0, r], to_twin)
+    send_ids(piece, id_send.at[0, 1], to_up)
+    send_ids(piece, id_send.at[1, 1], to_down)
+    send_ids(piece, id_send.at[2, 0], to_twin)
+
+    own_q, mate_q = q_buf.at[0:PIECE, :], q_buf.at[PIECE : 2 * PIECE, :]
+    for r in range(4):
+        wait_recv(landing(piece, r)[3], u_recv.at[r, 3])
+    remote(own_q, mate_q, y_send.at[0, 0], q_recv, to_mate).start()
+    send_whole(piece, 1, to_mate)
 
     def ids_of(j):
         return jnp.concatenate([id_slots[j, r] for r in range(4)], axis=1).astype(F32)
 
-    own_ids = ids_of(piece)
     eye = lax.broadcasted_iota(jnp.int32, (TILE, TILE), 0) == lax.broadcasted_iota(
         jnp.int32, (TILE, TILE), 1
     )
-    for r in range(4):
-        row = jnp.broadcast_to(own_ids[:, r * TILE : (r + 1) * TILE], (TILE, TILE))
-        column = jnp.sum(jnp.where(eye, row, 0.0), axis=1, keepdims=True)
-        q_id[r * TILE : (r + 1) * TILE, :] = jnp.broadcast_to(column, (TILE, TILE))
-    for r in range(4):
-        wait_recv(landing(piece, r)[3], u_recv.at[r, 3])
+
+    def column_from(row):
+        column = jnp.sum(
+            jnp.where(eye, jnp.broadcast_to(row, (TILE, TILE)), 0.0), axis=1, keepdims=True
+        )
+        return jnp.broadcast_to(column, (TILE, TILE))
+
+    def row_from(column):
+        return jnp.sum(jnp.where(eye, column, 0.0), axis=0, keepdims=True)
+
+    def set_query_ids(first, j):
+        found = ids_of(j)
+        for r in range(4):
+            q_id[first + r * TILE : first + (r + 1) * TILE, :] = column_from(
+                found[:, r * TILE : (r + 1) * TILE]
+            )
+
+    set_query_ids(0, piece)
 
     factor = HD ** -0.5 * 1.4426950408889634
 
@@ -176,7 +189,7 @@
         keys = slots[j, :, 0:HD]
         values = jnp.concatenate([slots[j, :, HD : 2 * HD], jnp.ones((PIECE, HD), BF16)], axis=1)
         key_ids = ids_of(j)
-        for r in range(4):
+        for r in range(4 if near_by else 8):
             rows = slice(r * TILE, (r + 1) * TILE)
             scores = lax.dot_general(
                 q_buf[rows, :], keys, (((1,), (1,)), ((), ())), preferred_element_type=F32
@@ -195,67 +208,129 @@
                 accumulate(jnp.where(window, scores, NEG), values, rows, m_l, acc_l)
             accumulate(jnp.where(same, scores, NEG), values, rows, m_r, acc_r)
 
+    mate_piece = slot_of(0, c, 1 - par)
+    before_mate = 2 * ((piece // 2 + 2 * nz - 1) % (2 * nz)) + 1 - par
+
     def turn(t, carry):
-        s, k = t // 6, t % 6
-        d, from_twin = k % 3, k // 3
-        dz, flip = step_of(s, d)
-        later = (s > 0).astype(jnp.int32)
-        j = slot_of(dz * later, flip * later) + from_twin * (2 - 4 * c)
-        used = jnp.logical_or(s > 0, d == 0)
-
-        @pl.when(jnp.logical_and(used, from_twin == 1))
-        def _():
-            wait_recv(id_slots.at[j], id_recv.at[j])
+        s, k = t // 5, t % 5
+        extra = k == 2
+        from_twin = (k > 2).astype(jnp.int32)
+        upward = (k == 1) | (k == 4)
+        core = c + from_twin * (1 - 2 * c)
+        j = slot_of(jnp.where(upward, s, -s), core, par)
+        j = jnp.where(extra, jnp.where(s == 2, mate_piece, before_mate), j)
+        used = jnp.where(extra, (s == 2) | (s == 3), jnp.logical_not(upward) | ((s > 0) & (s < 4)))
+
+        @pl.when((t == 5))
+        def _():
+            wait_recv(mate_q, q_recv)
+            wait_recv(id_slots.at[mate_piece], id_recv.at[mate_piece])
+            set_query_ids(PIECE, mate_piece)
+
+        @pl.when(used & (from_twin == 1))
+        def _():
+            wait_whole(j)
+
+        @pl.when((s == 1) & (k == 3) & (c == 0))
+        def _():
+            send_whole(j, 2, to_mate)
+
+        @pl.when(extra & (s == 2))
+        def _():
             for sub in range(SUBS):
                 wait_recv(sub_of(j, sub), ag_recv.at[j, sub])
 
+            @pl.when(c == 0)
+            def _():
+                send_whole(j, 3, to_twin)
+
+        @pl.when(extra & (s == 3))
+        def _():
+            wait_whole(j)
+
         back = piece // 2 - j // 2
 
-        @pl.when(jnp.logical_and(used, jnp.logical_and(back >= 0, back <= 1)))
+        @pl.when(used & (back >= 0) & (back <= 1))
         def _():
             attend(j, True)
 
-        @pl.when(jnp.logical_and(used, back > 1))
+        @pl.when(used & (back > 1))
         def _():
             attend(j, False)
 
-        @pl.when(jnp.logical_and(s < STEPS, d != 1))
-        def _():
-            sub = (2 * k) // 3
-            arrived = [slot_of(*step_of(s + 1, e)) for e in range(3)]
-            onward = source_slots(s + 2)
-            for e in range(3):
-                wait_recv(sub_of(arrived[e], sub), ag_recv.at[arrived[e], sub])
-
-            @pl.when(s + 1 < STEPS)
+        @pl.when((s < STEPS) & jnp.logical_not(extra))
+        def _():
+            sub = k - (k > 2).astype(jnp.int32)
+            n = s + 1
+            low, high = slot_of(-n, c, par), slot_of(n, c, par)
+            lower, upper = sub < 2, sub >= 2
+
+            @pl.when((n < STEPS) | lower)
             def _():
-                for e in range(3):
-                    send(onward[e], e, s + 2, sub, targets[e])
-
-            for e in range(3):
-                send(arrived[e], 3 + e, s + 1, sub, (z, y, twin, x))
+                wait_recv(sub_of(low, sub), ag_recv.at[low, sub])
+
+                @pl.when((n + 1 < STEPS) | ((n + 1 == STEPS) & lower))
+                def _():
+                    send(low, sub, ag_send.at[0, n + 1, sub], to_up)
+
+                send(low, sub, ag_send.at[2, n, sub], to_twin)
+
+            @pl.when((n < STEPS) | upper)
+            def _():
+                wait_recv(sub_of(high, sub), ag_recv.at[high, sub])
+
+                @pl.when((n + 1 < STEPS) | ((n + 1 == STEPS) & upper))
+                def _():
+                    send(high, sub, ag_send.at[1, n + 1, sub], to_down)
+
+                send(high, sub, ag_send.at[3, n, sub], to_twin)
 
             @pl.when(sub == 0)
             def _():
-                for e in range(3):
-                    wait_recv(id_slots.at[arrived[e]], id_recv.at[arrived[e]])
-
-                @pl.when(s + 1 < STEPS)
+                wait_recv(id_slots.at[low], id_recv.at[low])
+                send_ids(low, id_send.at[2, n], to_twin)
+
+                @pl.when(n < STEPS)
                 def _():
-                    for e in range(3):
-                        send_ids(onward[e], e, s + 2, targets[e])
-
-                for e in range(3):
-                    send_ids(arrived[e], 3 + e, s + 1, (z, y, twin, x))
+                    wait_recv(id_slots.at[high], id_recv.at[high])
+                    send_ids(low, id_send.at[0, n + 1], to_up)
+                    send_ids(high, id_send.at[3, n], to_twin)
+
+                    @pl.when(n + 1 < STEPS)
+                    def _():
+                        send_ids(high, id_send.at[1, n + 1], to_down)
 
         return carry
 
-    lax.fori_loop(0, 6 * (STEPS + 1), turn, 0)
+    lax.fori_loop(0, 5 * (STEPS + 1), turn, 0)
+
+    for r in range(4):
+        rows = slice(PIECE + r * TILE, PIECE + (r + 1) * TILE)
+        stats[2 * r : 2 * r + 1, :] = row_from(m_r[rows, :])
+        stats[2 * r + 1 : 2 * r + 2, :] = row_from(acc_r[rows, HD : 2 * HD])
+    remote(stats, stats_in, o_send.at[4], o_recv.at[4], to_mate).start()
+    for r in range(4):
+        rows = slice(PIECE + r * TILE, PIECE + (r + 1) * TILE)
+        here_rows = slice(r * TILE, (r + 1) * TILE)
+        weight = jnp.maximum(acc_r[rows, HD : 2 * HD], 1e-30)
+        o_away[here_rows, :] = (acc_r[rows, 0:HD] / weight).astype(BF16)
+        remote(
+            o_away.at[here_rows, :], o_in.at[here_rows, :], o_send.at[r], o_recv.at[r], to_mate
+        ).start()
+    wait_recv(stats_in, o_recv.at[4])
 
     columns = pl.ds(pl.multiple_of(head * HD, HD), HD)
     for r, (yy, cc) in enumerate(sources):
         rows = slice(r * TILE, (r + 1) * TILE)
-        routed = (acc_r[rows, 0:HD] / acc_r[rows, HD : 2 * HD]).astype(BF16).astype(F32)
+        wait_recv(o_in.at[rows, :], o_recv.at[r])
+        m_here, m_there = m_r[rows, :], column_from(stats_in[2 * r : 2 * r + 1, :])
+        largest = jnp.maximum(m_here, m_there)
+        kept = jnp.exp2(m_here - largest)
+        added = jnp.exp2(m_there - largest) * column_from(stats_in[2 * r + 1 : 2 * r + 2, :])
+        routed = (acc_r[rows, 0:HD] * kept + o_in[rows, :].astype(F32) * added) / (
+            acc_r[rows, HD : 2 * HD] * kept + added
+        )
+        routed = routed.astype(BF16).astype(F32)
         local = acc_l[rows, 0:HD] / acc_l[rows, HD : 2 * HD]
         o_buf[rows, :] = (routed + local).astype(BF16)
         remote(
@@ -306,18 +381,41 @@
             wait_send(ref, u_send.at[i, t])
     for r in range(4):
         wait_send(o_buf.at[r * TILE : (r + 1) * TILE, :], ret_send.at[r])
-    wait_send(id_slots.at[0], id_send.at[3, 0])
+    for r in range(4):
+        wait_send(o_away.at[r * TILE : (r + 1) * TILE, :], o_send.at[r])
+    wait_send(stats, o_send.at[4])
+    wait_send(own_q, y_send.at[0, 0])
+
+    def sent_whole(n):
+        for sub in range(SUBS):
+            wait_send(sub_of(0, sub), y_send.at[n, sub])
+        wait_send(id_slots.at[0], y_send.at[n, SUBS])
+
+    sent_whole(1)
+
+    @pl.when(c == 0)
+    def _():
+        sent_whole(2)
+        sent_whole(3)
+
+    wait_send(id_slots.at[0], id_send.at[2, 0])
     for sub in range(SUBS):
-        wait_send(sub_of(0, sub), ag_send.at[3, 0, sub])
+        wait_send(sub_of(0, sub), ag_send.at[2, 0, sub])
 
     def settle(s, carry):
-        for d in range(6):
+        for d in range(4):
             wait_send(id_slots.at[0], id_send.at[d, s])
             for sub in range(SUBS):
                 wait_send(sub_of(0, sub), ag_send.at[d, s, sub])
         return carry
 
-    lax.fori_loop(1, STEPS + 1, settle, 0)
+    lax.fori_loop(1, STEPS, settle, 0)
+    for d in (0, 2):
+        wait_send(id_slots.at[0], id_send.at[d, STEPS])
+    for d in range(4):
+        for sub in range(2):
+            n = sub + 2 * (d % 2)
+            wait_send(sub_of(0, n), ag_send.at[d, STEPS, n])
     for e in range(2):
         for n in range(3):
             wait_send(relay_out.at[e], rs_send.at[e, n])
@@ -333,28 +431,36 @@
         in_specs=[anywhere] * 4 + [pl.BlockSpec(memory_space=pltpu.SMEM)],
         out_specs=pl.BlockSpec(memory_space=pltpu.VMEM),
         scratch_shapes=[
-            pltpu.VMEM((PIECE, HD), BF16),
+            pltpu.VMEM((2 * PIECE, HD), BF16),
             pltpu.VMEM((32, PIECE, 2 * HD), BF16),
             pltpu.VMEM((1, TILE), jnp.int32),
             pltpu.VMEM((32, 4, 1, TILE), jnp.int32),
             pltpu.VMEM((PIECE, HD), BF16),
+            pltpu.VMEM((PIECE, HD), BF16),
+            pltpu.VMEM((PIECE, HD), BF16),
+            pltpu.VMEM((8, TILE), F32),
+            pltpu.VMEM((8, TILE), F32),
             pltpu.VMEM((tokens, width), BF16),
             pltpu.VMEM(out_weight.shape, BF16),
             pltpu.VMEM((3, tokens, width), BF16),
             pltpu.VMEM((2, tokens // 2, width), BF16),
             pltpu.VMEM((2, tokens // 2, width), BF16),
             pltpu.VMEM((2, tokens, width), BF16),
+            pltpu.VMEM((2 * PIECE, HD), F32),
             pltpu.VMEM((PIECE, HD), F32),
-            pltpu.VMEM((PIECE, HD), F32),
+            pltpu.VMEM((2 * PIECE, 2 * HD), F32),
             pltpu.VMEM((PIECE, 2 * HD), F32),
-            pltpu.VMEM((PIECE, 2 * HD), F32),
-            pltpu.VMEM((PIECE, HD), F32),
+            pltpu.VMEM((2 * PIECE, HD), F32),
             dma((4, 4)),
             dma((4, 4)),
-            dma((6, STEPS + 1, SUBS)),
+            dma((4, STEPS + 1, SUBS)),
             dma((32, SUBS)),
-            dma((6, STEPS + 1)),
+            dma((4, STEPS + 1)),
             dma((32,)),
+            dma((4, SUBS + 1)),
+            dma,
+            dma((5,)),
+            dma((5,)),
             dma((4,)),
             dma((4,)),
             dma((2, 3)),

time: 75.1 us -> 70.6 us (0.940)
  Pallas kernels: 73.1 us -> 68.3 us
    pallas_call x1, Pallas kernels: 73.1 us -> 68.3 us  [body(): pl.pallas_call(kernel, out_shape=jax.ShapeDtypeStruct((tokens, width), BF...]
where the time goes in v3:
time: 70.6 us; the launch traced here: 69.9 us
  Pallas kernels  68.3 us (97%)
  local copies, waits for them, and re-layouts  1.57 us (2%)
    pallas_call x1, Pallas kernels, body(): pl.pallas_call(kernel, out_shape=jax.ShapeDtypeStruct((tokens, width), BF...  68.3 us
    unnamed x1, local copies, waits for them, and re-layouts  1.57 us

profile of v3, /device:TPU:1, one launch (start us, length us, event | category | flops | bytes accessed | tf_op | source)
XLA Modules:
  0.0 69.9 jit_solution(4292943863128292070)
XLA Ops:
  0.0 68.3 %attention.1 = bf16[128,512]{1,0:T(8,128)(2,1)} custom-call(bf16[128,512]{1,0:T(8,128)(2,1)} %q_in.1, bf16[128,512]{1,0:T(8,128)(2,1)} %k_in.1, bf16[128,512]{1,0:T(8,128)(2,1)} %v_in.1, bf16[512,2048]{1,0:T(8,128)(2,1)} %w_in.1, s32[1,16]{1,0:T(1,128)} %id_in.1), custom_call_target="tpu_custom_call" | custom-call | tf_op jit(solution)/shard_map/attention/pallas_call | solution.py:428
  68.3 1.6 %copy.7 = bf16[128,512]{1,0:T(8,128)(2,1)} copy(bf16[128,512]{1,0:T(8,128)(2,1)} %attention.1) | data formatting | bytes 262144

commit v4 on v3

--- a/solution.py
+++ b/solution.py
@@ -23,9 +23,9 @@
 def kernel(
     q_in, k_in, v_in, w_in, id_in, out_ref,
     q_buf, slots, id_row, id_slots, o_buf, o_away, o_in, stats, stats_in, att, w_buf,
-    part, relay_out, relay_in, parts_in, m_r, m_l, acc_r, acc_l, q_id,
+    m_r, m_l, acc_r, acc_l, q_id,
     u_send, u_recv, ag_send, ag_recv, id_send, id_recv, y_send, q_recv, o_send, o_recv,
-    ret_send, ret_recv, rs_send, rs_recv, w_sem,
+    ret_send, ret_recv, x_send, x_recv, w_send, w_recv,
 ):
     z, y, c = (lax.axis_index(a) for a in SEQ)
     x = lax.axis_index("head")
@@ -37,8 +37,9 @@
     place = 2 * ((y // 2) % 2) + c
     head = y // 2
     z_up, z_down = (z + 1) % nz, (z + nz - 1) % nz
-    x_up, x_down = (x + 1) % nx, (x + nx - 1) % nx
-    dests = [(y + far) % ny for far in (3, ny - 3, 1, ny - 1)]
+    x_up, x_down, x_far = (x + 1) % nx, (x + nx - 1) % nx, (x + 2) % nx
+    dests = [(y + far) % ny for far in (1, ny - 1, 3, ny - 3)]
+    first = 2 * ((1 - par + 4 * c - y + 2 * ny) % ny == 5).astype(jnp.int32)
     sources = [(1 - par + 4 * c + 2 * (r // 2), r % 2) for r in range(4)]
 
     def remote(src, dst, send_sem, recv_sem, to):
@@ -58,12 +59,14 @@
     barrier = pltpu.get_barrier_semaphore()
     near = [(z, yy, y // 4, x) for yy in dests] + [(z, yy, cc, x) for yy, cc in sources]
     near += [(z_up, y, c, x), (z_down, y, c, x), (z, mate, c, x), (z, y, twin, x)]
-    near += [(z, y, c, x_up), (z, y, c, x_down)]
+    near += [(z, y, c, x_up), (z, y, c, x_down), (z, y, c, x_far)]
     for to in near:
         pl.semaphore_signal(barrier, 1, device_id=to, device_id_type=MESH)
 
-    w_copy = pltpu.make_async_copy(w_in, w_buf, w_sem)
-    w_copy.start()
+    def w_columns(to):
+        return w_in.at[:, pl.ds(pl.multiple_of(to * 4 * HD, 4 * HD), 4 * HD)]
+
+    pltpu.make_async_copy(w_columns(x), w_buf.at[x], w_recv.at[0]).start()
     block_of = lax.broadcasted_iota(jnp.int32, (1, TILE), 1) // BLOCK
     row = jnp.zeros((1, TILE), jnp.int32)
     for b in range(TILE // BLOCK):
@@ -100,6 +103,11 @@
                     (z, yy, y // 4, x),
                 ).start()
 
+    for d, to in enumerate((x_up, x_down, x_far)):
+        remote(
+            w_columns(to), w_buf.at[x], w_send.at[d], w_recv.at[1 + d], (z, y, c, to)
+        ).start()
+
     def slot_of(dz, core, p):
         return 4 * ((z + dz + nz) % nz) + 2 * core + p
 
@@ -125,7 +133,8 @@
         for sub in range(SUBS):
             wait_recv(sub_of(j, sub), ag_recv.at[j, sub])
 
-    for r in range(4):
+    for n in range(4):
+        r = (first + n) % 4
         landed = landing(piece, r)
         for t in range(3):
             wait_recv(landed[t], u_recv.at[r, t])
@@ -260,7 +269,8 @@
 
         @pl.when((s < STEPS) & jnp.logical_not(extra))
         def _():
-            sub = k - (k > 2).astype(jnp.int32)
+            order = k - (k > 2).astype(jnp.int32)
+            sub = (first + order) % 4
             n = s + 1
             low, high = slot_of(-n, c, par), slot_of(n, c, par)
             lower, upper = sub < 2, sub >= 2
@@ -285,7 +295,7 @@
 
                 send(high, sub, ag_send.at[3, n, sub], to_twin)
 
-            @pl.when(sub == 0)
+            @pl.when(order == 0)
             def _():
                 wait_recv(id_slots.at[low], id_recv.at[low])
                 send_ids(low, id_send.at[2, n], to_twin)
@@ -334,47 +344,44 @@
         local = acc_l[rows, 0:HD] / acc_l[rows, HD : 2 * HD]
         o_buf[rows, :] = (routed + local).astype(BF16)
         remote(
-            o_buf.at[rows, :], att.at[:, columns], ret_send.at[r], ret_recv.at[head],
+            o_buf.at[rows, :], att.at[x, :, columns], ret_send.at[r], ret_recv.at[head],
             (z, yy, cc, x),
         ).start()
 
-    w_copy.wait()
-    for i in range(4):
-        wait_recv(att.at[:, i * HD : (i + 1) * HD], ret_recv.at[i])
-
-    def partial(column_of):
-        columns = pl.ds(pl.multiple_of(column_of * 4 * HD, 4 * HD), 4 * HD)
-        return jnp.dot(att[...], w_buf[:, columns], preferred_element_type=F32)
-
-    low, high = slice(0, TILE // 2), slice(TILE // 2, TILE)
-    sides = ((x_up, low, high), (x_down, high, low))
-    part[2] = partial((x + 2) % nx).astype(BF16)
-    for e, (to, passed, _) in enumerate(sides):
-        remote(
-            part.at[2, passed, :], relay_in.at[e], rs_send.at[e, 0], rs_recv.at[e, 0], (z, y, c, to)
-        ).start()
-    sums = []
-    for e, (to, passed, direct) in enumerate(sides):
-        here_sum = partial(to)
-        part[e] = here_sum.astype(BF16)
-        remote(
-            part.at[e, direct, :], parts_in.at[e, direct, :], rs_send.at[e, 1], rs_recv.at[e, 1],
-            (z, y, c, to),
-        ).start()
-        sums.append(here_sum[passed, :])
-    total = partial(x)
-    for e, (to, passed, direct) in enumerate(sides):
-        wait_recv(relay_in.at[e], rs_recv.at[e, 0])
-        relay_out[e] = (sums[e] + relay_in[e].astype(F32)).astype(BF16)
-        remote(
-            relay_out.at[e], parts_in.at[e, passed, :], rs_send.at[e, 2], rs_recv.at[e, 2],
-            (z, y, c, to),
-        ).start()
-    for e, (to, passed, direct) in enumerate(sides):
-        wait_recv(parts_in.at[e, direct, :], rs_recv.at[e, 1])
-    for e, (to, passed, direct) in enumerate(sides):
-        wait_recv(parts_in.at[e, passed, :], rs_recv.at[e, 2])
-    out_ref[...] = (total + parts_in[0].astype(F32) + parts_in[1].astype(F32)).astype(BF16)
+    def block(plane, n):
+        lanes = pl.ds(pl.multiple_of((dests[n] // 2) * HD, HD), HD)
+        return att.at[plane, :, lanes]
+
+    def pass_on(plane, n, way, slot, to):
+        ref = block(plane, n)
+        remote(ref, ref, x_send.at[way, n], x_recv.at[slot, n], (z, y, c, to)).start()
+
+    def project(plane):
+        return jnp.dot(att[plane], w_buf[plane], preferred_element_type=F32)
+
+    for n in range(4):
+        wait_recv(block(x, n), ret_recv.at[dests[n] // 2])
+        pass_on(x, n, 0, 0, x_up)
+        pass_on(x, n, 1, 1, x_down)
+    for d, plane in enumerate((x, x_down, x_up, x_far)):
+        wait_recv(w_buf.at[plane], w_recv.at[d])
+    total = project(x)
+    for n in range(4):
+        if n % 2 == 0:
+            wait_recv(block(x_down, n), x_recv.at[0, n])
+            pass_on(x_down, n, 2, 2, x_up)
+        else:
+            wait_recv(block(x_up, n), x_recv.at[1, n])
+            pass_on(x_up, n, 2, 2, x_down)
+    for n in (1, 3):
+        wait_recv(block(x_down, n), x_recv.at[0, n])
+    total = total + project(x_down)
+    for n in (0, 2):
+        wait_recv(block(x_up, n), x_recv.at[1, n])
+    total = total + project(x_up)
+    for n in range(4):
+        wait_recv(block(x_far, n), x_recv.at[2, n])
+    out_ref[...] = total + project(x_far)
 
     for i, yy in enumerate(dests):
         for t, ref in enumerate(leaving(yy)):
@@ -416,18 +423,19 @@
         for sub in range(2):
             n = sub + 2 * (d % 2)
             wait_send(sub_of(0, n), ag_send.at[d, STEPS, n])
-    for e in range(2):
-        for n in range(3):
-            wait_send(relay_out.at[e], rs_send.at[e, n])
+    for d in range(3):
+        wait_send(w_buf.at[0], w_send.at[d])
+        for n in range(4):
+            wait_send(block(0, n), x_send.at[d, n])
 
 
 def body(query_rows, key_rows, value_rows, out_weight, cluster_ids):
     tokens, width = query_rows.shape
     dma = pltpu.SemaphoreType.DMA
     anywhere = pl.BlockSpec(memory_space=pl.ANY)
-    return pl.pallas_call(
+    total = pl.pallas_call(
         kernel,
-        out_shape=jax.ShapeDtypeStruct((tokens, width), BF16),
+        out_shape=jax.ShapeDtypeStruct((tokens, width), F32),
         in_specs=[anywhere] * 4 + [pl.BlockSpec(memory_space=pltpu.SMEM)],
         out_specs=pl.BlockSpec(memory_space=pltpu.VMEM),
         scratch_shapes=[
@@ -440,12 +448,8 @@
             pltpu.VMEM((PIECE, HD), BF16),
             pltpu.VMEM((8, TILE), F32),
             pltpu.VMEM((8, TILE), F32),
-            pltpu.VMEM((tokens, width), BF16),
-            pltpu.VMEM(out_weight.shape, BF16),
-            pltpu.VMEM((3, tokens, width), BF16),
-            pltpu.VMEM((2, tokens // 2, width), BF16),
-            pltpu.VMEM((2, tokens // 2, width), BF16),
-            pltpu.VMEM((2, tokens, width), BF16),
+            pltpu.VMEM((4, tokens, width), BF16),
+            pltpu.VMEM((4, width, width), BF16),
             pltpu.VMEM((2 * PIECE, HD), F32),
             pltpu.VMEM((PIECE, HD), F32),
             pltpu.VMEM((2 * PIECE, 2 * HD), F32),
@@ -463,13 +467,15 @@
             dma((5,)),
             dma((4,)),
             dma((4,)),
-            dma((2, 3)),
-            dma((2, 3)),
-            dma,
+            dma((3, 4)),
+            dma((3, 4)),
+            dma((3,)),
+            dma((4,)),
         ],
         compiler_params=pltpu.CompilerParams(collective_id=0, has_side_effects=True),
         name="attention",
     )(query_rows, key_rows, value_rows, out_weight, cluster_ids)
+    return total.astype(BF16)
 
 
 def solution(mesh):

time: 70.6 us -> 72.2 us (1.023)
  the two profiles are of different devices: /device:TPU:1 before, /device:TPU:448 now
where the time goes in v4:
time: 72.2 us; the launch traced here: 72.1 us
  Pallas kernels  70.4 us (98%)
  other arithmetic  1.62 us (2%)
    pallas_call x1, Pallas kernels, body(): pl.pallas_call(kernel, out_shape=jax.ShapeDtypeStruct((tokens, width), F3...  70.4 us
    convert_element_type x1, other arithmetic, body(): return total.astype(BF16)  1.62 us

profile of v4, /device:TPU:448, one launch (start us, length us, event | category | flops | bytes accessed | tf_op | source)
XLA Modules:
  0.0 72.1 jit_solution(11639770823258669827)
XLA Ops:
  0.0 70.4 %attention.1 = f32[128,512]{1,0:T(8,128)} custom-call(bf16[128,512]{1,0:T(8,128)(2,1)} %q_in.1, bf16[128,512]{1,0:T(8,128)(2,1)} %k_in.1, bf16[128,512]{1,0:T(8,128)(2,1)} %v_in.1, bf16[512,2048]{1,0:T(8,128)(2,1)} %w_in.1, s32[1,16]{1,0:T(1,128)} %id_in.1), custom_call_target="tpu_custom_call" | custom-call | tf_op jit(solution)/shard_map/attention/pallas_call | solution.py:436
  70.4 1.6 %convert_element_type.3 = bf16[128,512]{1,0:T(8,128)(2,1)} convert(f32[128,512]{1,0:T(8,128)} %attention.1) | non-fusion elementwise | flops 65536 | bytes 393216 | tf_op jit(solution)/shard_map/convert_element_type | solution.py:478

commit v5 on v4

--- a/solution.py
+++ b/solution.py
@@ -145,6 +145,52 @@
     send_ids(piece, id_send.at[1, 1], to_down)
     send_ids(piece, id_send.at[2, 0], to_twin)
 
+    def forward(n, order):
+        sub = (first + order) % 4
+        low, high = slot_of(-n, c, par), slot_of(n, c, par)
+        lower, upper = sub < 2, sub >= 2
+
+        @pl.when((n < STEPS) | lower)
+        def _():
+            wait_recv(sub_of(low, sub), ag_recv.at[low, sub])
+
+            @pl.when((n + 1 < STEPS) | ((n + 1 == STEPS) & lower))
+            def _():
+                send(low, sub, ag_send.at[0, n + 1, sub], to_up)
+
+            send(low, sub, ag_send.at[2, n, sub], to_twin)
+
+        @pl.when((n < STEPS) | upper)
+        def _():
+            wait_recv(sub_of(high, sub), ag_recv.at[high, sub])
+
+            @pl.when((n + 1 < STEPS) | ((n + 1 == STEPS) & upper))
+            def _():
+                send(high, sub, ag_send.at[1, n + 1, sub], to_down)
+
+            send(high, sub, ag_send.at[3, n, sub], to_twin)
+
+        @pl.when(order == 0)
+        def _():
+            wait_recv(id_slots.at[low], id_recv.at[low])
+            send_ids(low, id_send.at[2, n], to_twin)
+
+            @pl.when(n < STEPS)
+            def _():
+                wait_recv(id_slots.at[high], id_recv.at[high])
+                send_ids(low, id_send.at[0, n + 1], to_up)
+                send_ids(high, id_send.at[3, n], to_twin)
+
+                @pl.when(n + 1 < STEPS)
+                def _():
+                    send_ids(high, id_send.at[1, n + 1], to_down)
+
+    def forward_first(order, carry):
+        forward(jnp.int32(1), order)
+        return carry
+
+    lax.fori_loop(0, 2, forward_first, 0)
+
     own_q, mate_q = q_buf.at[0:PIECE, :], q_buf.at[PIECE : 2 * PIECE, :]
     for r in range(4):
         wait_recv(landing(piece, r)[3], u_recv.at[r, 3])
@@ -194,12 +240,12 @@
     def start_of(j):
         return 1024 * (j // 2) + 256 * (1 - j % 2)
 
-    def attend(j, near_by):
+    def attend(j, base, near_by):
         keys = slots[j, :, 0:HD]
         values = jnp.concatenate([slots[j, :, HD : 2 * HD], jnp.ones((PIECE, HD), BF16)], axis=1)
         key_ids = ids_of(j)
-        for r in range(4 if near_by else 8):
-            rows = slice(r * TILE, (r + 1) * TILE)
+        for r in range(4):
+            rows = slice(base + r * TILE, base + (r + 1) * TILE)
             scores = lax.dot_general(
                 q_buf[rows, :], keys, (((1,), (1,)), ((), ())), preferred_element_type=F32
             ) * factor
@@ -223,6 +269,8 @@
     def turn(t, carry):
         s, k = t // 5, t % 5
         extra = k == 2
+        order = jnp.where(s == 0, k + 2, k - (k > 2).astype(jnp.int32))
+        moves = jnp.where(s == 0, k < 2, (s < STEPS) & (k != 2))
         from_twin = (k > 2).astype(jnp.int32)
         upward = (k == 1) | (k == 4)
         core = c + from_twin * (1 - 2 * c)
@@ -230,7 +278,11 @@
         j = jnp.where(extra, jnp.where(s == 2, mate_piece, before_mate), j)
         used = jnp.where(extra, (s == 2) | (s == 3), jnp.logical_not(upward) | ((s > 0) & (s < 4)))
 
-        @pl.when((t == 5))
+        @pl.when((s == 1) & moves)
+        def _():
+            forward(s + 1, order)
+
+        @pl.when(t == 5)
         def _():
             wait_recv(mate_q, q_recv)
             wait_recv(id_slots.at[mate_piece], id_recv.at[mate_piece])
@@ -261,58 +313,32 @@
 
         @pl.when(used & (back >= 0) & (back <= 1))
         def _():
-            attend(j, True)
+            attend(j, 0, True)
 
         @pl.when(used & (back > 1))
         def _():
-            attend(j, False)
-
-        @pl.when((s < STEPS) & jnp.logical_not(extra))
-        def _():
-            order = k - (k > 2).astype(jnp.int32)
-            sub = (first + order) % 4
-            n = s + 1
-            low, high = slot_of(-n, c, par), slot_of(n, c, par)
-            lower, upper = sub < 2, sub >= 2
-
-            @pl.when((n < STEPS) | lower)
-            def _():
-                wait_recv(sub_of(low, sub), ag_recv.at[low, sub])
-
-                @pl.when((n + 1 < STEPS) | ((n + 1 == STEPS) & lower))
-                def _():
-                    send(low, sub, ag_send.at[0, n + 1, sub], to_up)
-
-                send(low, sub, ag_send.at[2, n, sub], to_twin)
-
-            @pl.when((n < STEPS) | upper)
-            def _():
-                wait_recv(sub_of(high, sub), ag_recv.at[high, sub])
-
-                @pl.when((n + 1 < STEPS) | ((n + 1 == STEPS) & upper))
-                def _():
-                    send(high, sub, ag_send.at[1, n + 1, sub], to_down)
-
-                send(high, sub, ag_send.at[3, n, sub], to_twin)
-
-            @pl.when(order == 0)
-            def _():
-                wait_recv(id_slots.at[low], id_recv.at[low])
-                send_ids(low, id_send.at[2, n], to_twin)
-
-                @pl.when(n < STEPS)
-                def _():
-                    wait_recv(id_slots.at[high], id_recv.at[high])
-                    send_ids(low, id_send.at[0, n + 1], to_up)
-                    send_ids(high, id_send.at[3, n], to_twin)
-
-                    @pl.when(n + 1 < STEPS)
-                    def _():
-                        send_ids(high, id_send.at[1, n + 1], to_down)
+            attend(j, PIECE, False)
+            attend(j, 0, False)
+
+        @pl.when((s != 1) & moves)
+        def _():
+            forward(s + 1, order)
 
         return carry
 
-    lax.fori_loop(0, 5 * (STEPS + 1), turn, 0)
+    lax.fori_loop(0, 5 * STEPS, turn, 0)
+
+    last_own, last_twin = slot_of(STEPS, c, par), slot_of(STEPS, twin, par)
+
+    def attend_far(j, base):
+        @pl.when(piece // 2 - j // 2 > 1)
+        def _():
+            attend(j, base, False)
+
+    attend_far(last_own, PIECE)
+    attend_far(last_own, 0)
+    wait_whole(last_twin)
+    attend_far(last_twin, PIECE)
 
     for r in range(4):
         rows = slice(PIECE + r * TILE, PIECE + (r + 1) * TILE)
@@ -327,6 +353,7 @@
         remote(
             o_away.at[here_rows, :], o_in.at[here_rows, :], o_send.at[r], o_recv.at[r], to_mate
         ).start()
+    attend_far(last_twin, 0)
     wait_recv(stats_in, o_recv.at[4])
 
     columns = pl.ds(pl.multiple_of(head * HD, HD), HD)

time: 72.2 us -> 73.7 us (1.021)
  the two profiles are of different devices: /device:TPU:448 before, /device:TPU:16 now
where the time goes in v5:
time: 73.7 us; the launch traced here: 73.6 us
  Pallas kernels  72 us (98%)
  other arithmetic  1.62 us (2%)
    pallas_call x1, Pallas kernels, body(): pl.pallas_call(kernel, out_shape=jax.ShapeDtypeStruct((tokens, width), F3...  72 us
    convert_element_type x1, other arithmetic, body(): return total.astype(BF16)  1.62 us

profile of v5, /device:TPU:16, one launch (start us, length us, event | category | flops | bytes accessed | tf_op | source)
XLA Modules:
  0.0 73.6 jit_solution(12575721149129929208)
XLA Ops:
  0.0 72.0 %attention.1 = f32[128,512]{1,0:T(8,128)} custom-call(bf16[128,512]{1,0:T(8,128)(2,1)} %q_in.1, bf16[128,512]{1,0:T(8,128)(2,1)} %k_in.1, bf16[128,512]{1,0:T(8,128)(2,1)} %v_in.1, bf16[512,2048]{1,0:T(8,128)(2,1)} %w_in.1, s32[1,16]{1,0:T(1,128)} %id_in.1), custom_call_target="tpu_custom_call" | custom-call | tf_op jit(solution)/shard_map/attention/pallas_call | solution.py:463
  72.0 1.6 %convert_element_type.3 = bf16[128,512]{1,0:T(8,128)(2,1)} convert(f32[128,512]{1,0:T(8,128)} %attention.1) | non-fusion elementwise | flops 65536 | bytes 393216 | tf_op jit(solution)/shard_map/convert_element_type | solution.py:505

commit v6 on v5

--- a/solution.py
+++ b/solution.py
@@ -240,28 +240,33 @@
     def start_of(j):
         return 1024 * (j // 2) + 256 * (1 - j % 2)
 
-    def attend(j, base, near_by):
+    def attend(j, bases, kind):
         keys = slots[j, :, 0:HD]
         values = jnp.concatenate([slots[j, :, HD : 2 * HD], jnp.ones((PIECE, HD), BF16)], axis=1)
         key_ids = ids_of(j)
-        for r in range(4):
-            rows = slice(base + r * TILE, base + (r + 1) * TILE)
+        lane = lax.broadcasted_iota(jnp.int32, (1, PIECE), 1)
+        key_place = lane + jnp.where(lane >= 256, 256, 0) + (start_of(j) - start_of(piece))
+        query_row = lax.broadcasted_iota(jnp.int32, (TILE, TILE), 0)
+        for first_row in [base + r * TILE for base in bases for r in range(4)]:
+            rows = slice(first_row, first_row + TILE)
             scores = lax.dot_general(
                 q_buf[rows, :], keys, (((1,), (1,)), ((), ())), preferred_element_type=F32
             ) * factor
-            same = across_keys(q_id[rows, :]) == key_ids
-            if near_by:
-                lane = lax.broadcasted_iota(jnp.int32, (TILE, PIECE), 1)
-                ahead = (
-                    start_of(j) - start_of(piece) - r * TILE - 256 * (r // 2)
-                    + lane + jnp.where(lane >= 256, 256, 0)
-                    - lax.broadcasted_iota(jnp.int32, (TILE, PIECE), 0)
-                )
-                causal = ahead <= 0
-                same = jnp.logical_and(same, causal)
-                window = jnp.logical_and(causal, ahead > -WINDOW)
-                accumulate(jnp.where(window, scores, NEG), values, rows, m_l, acc_l)
-            accumulate(jnp.where(same, scores, NEG), values, rows, m_r, acc_r)
+            if kind == "far":
+                allowed = across_keys(q_id[rows, :]) == key_ids
+            else:
+                query_place = first_row + 256 * (first_row // 256)
+                ahead = (key_place - query_place) - across_keys(query_row)
+                allowed = ahead <= 0
+                if kind == "near":
+                    allowed = allowed & (across_keys(q_id[rows, :]) == key_ids)
+                else:
+                    allowed = allowed & (ahead > -WINDOW)
+            scores = jnp.where(allowed, scores, NEG)
+            if kind == "local":
+                accumulate(scores, values, rows, m_l, acc_l)
+            else:
+                accumulate(scores, values, rows, m_r, acc_r)
 
     mate_piece = slot_of(0, c, 1 - par)
     before_mate = 2 * ((piece // 2 + 2 * nz - 1) % (2 * nz)) + 1 - par
@@ -313,12 +318,11 @@
 
         @pl.when(used & (back >= 0) & (back <= 1))
         def _():
-            attend(j, 0, True)
+            attend(j, (0,), "near")
 
         @pl.when(used & (back > 1))
         def _():
-            attend(j, PIECE, False)
-            attend(j, 0, False)
+            attend(j, (PIECE, 0), "far")
 
         @pl.when((s != 1) & moves)
         def _():
@@ -333,7 +337,7 @@
     def attend_far(j, base):
         @pl.when(piece // 2 - j // 2 > 1)
         def _():
-            attend(j, base, False)
+            attend(j, (base,), "far")
 
     attend_far(last_own, PIECE)
     attend_far(last_own, 0)
@@ -354,6 +358,18 @@
             o_away.at[here_rows, :], o_in.at[here_rows, :], o_send.at[r], o_recv.at[r], to_mate
         ).start()
     attend_far(last_twin, 0)
+
+    def attend_local(n, carry):
+        half = piece // 2 - n // 2
+        j = 2 * jnp.maximum(half, 0) + (par + n) % 2
+
+        @pl.when(half >= 0)
+        def _():
+            attend(j, (0,), "local")
+
+        return carry
+
+    lax.fori_loop(0, 4, attend_local, 0)
     wait_recv(stats_in, o_recv.at[4])
 
     columns = pl.ds(pl.multiple_of(head * HD, HD), HD)

time: 73.7 us -> 71.2 us (0.966)
  the two profiles are of different devices: /device:TPU:16 before, /device:TPU:1 now
where the time goes in v6:
time: 71.2 us; the launch traced here: 70.2 us
  Pallas kernels  68.6 us (96%)
  other arithmetic  1.62 us (2%)
    pallas_call x1, Pallas kernels, body(): pl.pallas_call(kernel, out_shape=jax.ShapeDtypeStruct((tokens, width), F3...  68.6 us
    convert_element_type x1, other arithmetic, body(): return total.astype(BF16)  1.62 us

profile of v6, /device:TPU:1, one launch (start us, length us, event | category | flops | bytes accessed | tf_op | source)
XLA Modules:
  0.0 70.2 jit_solution(8238832908274962092)
XLA Ops:
  0.0 68.6 %attention.1 = f32[128,512]{1,0:T(8,128)} custom-call(bf16[128,512]{1,0:T(8,128)(2,1)} %q_in.1, bf16[128,512]{1,0:T(8,128)(2,1)} %k_in.1, bf16[128,512]{1,0:T(8,128)(2,1)} %v_in.1, bf16[512,2048]{1,0:T(8,128)(2,1)} %w_in.1, s32[1,16]{1,0:T(1,128)} %id_in.1), custom_call_target="tpu_custom_call" | custom-call | tf_op jit(solution)/shard_map/attention/pallas_call | solution.py:479
  68.6 1.6 %convert_element_type.3 = bf16[128,512]{1,0:T(8,128)(2,1)} convert(f32[128,512]{1,0:T(8,128)} %attention.1) | non-fusion elementwise | flops 65536 | bytes 393216 | tf_op jit(solution)/shard_map/convert_element_type | solution.py:521

commit v7 on v6

--- a/solution.py
+++ b/solution.py
@@ -320,6 +320,10 @@
         def _():
             attend(j, (0,), "near")
 
+            @pl.when(jnp.logical_not(extra))
+            def _():
+                attend(j, (0,), "local")
+
         @pl.when(used & (back > 1))
         def _():
             attend(j, (PIECE, 0), "far")
@@ -360,8 +364,8 @@
     attend_far(last_twin, 0)
 
     def attend_local(n, carry):
-        half = piece // 2 - n // 2
-        j = 2 * jnp.maximum(half, 0) + (par + n) % 2
+        half = piece // 2 - n
+        j = 2 * jnp.maximum(half, 0) + 1 - par
 
         @pl.when(half >= 0)
         def _():
@@ -369,7 +373,7 @@
 
         return carry
 
-    lax.fori_loop(0, 4, attend_local, 0)
+    lax.fori_loop(0, 2, attend_local, 0)
     wait_recv(stats_in, o_recv.at[4])
 
     columns = pl.ds(pl.multiple_of(head * HD, HD), HD)

time: 71.2 us -> 72 us (1.011)
  the two profiles are of different devices: /device:TPU:1 before, /device:TPU:17 now
where the time goes in v7:
time: 72 us; the launch traced here: 71.8 us
  Pallas kernels  70.2 us (98%)
  other arithmetic  1.62 us (2%)
    pallas_call x1, Pallas kernels, body(): pl.pallas_call(kernel, out_shape=jax.ShapeDtypeStruct((tokens, width), F3...  70.2 us
    convert_element_type x1, other arithmetic, body(): return total.astype(BF16)  1.62 us

profile of v7, /device:TPU:17, one launch (start us, length us, event | category | flops | bytes accessed | tf_op | source)
XLA Modules:
  0.0 71.8 jit_solution(14234813278652530211)
XLA Ops:
  0.0 70.2 %attention.1 = f32[128,512]{1,0:T(8,128)} custom-call(bf16[128,512]{1,0:T(8,128)(2,1)} %q_in.1, bf16[128,512]{1,0:T(8,128)(2,1)} %k_in.1, bf16[128,512]{1,0:T(8,128)(2,1)} %v_in.1, bf16[512,2048]{1,0:T(8,128)(2,1)} %w_in.1, s32[1,16]{1,0:T(1,128)} %id_in.1), custom_call_target="tpu_custom_call" | custom-call | tf_op jit(solution)/shard_map/attention/pallas_call | solution.py:483
  70.2 1.6 %convert_element_type.3 = bf16[128,512]{1,0:T(8,128)(2,1)} convert(f32[128,512]{1,0:T(8,128)} %attention.1) | non-fusion elementwise | flops 65536 | bytes 393216 | tf_op jit(solution)/shard_map/convert_element_type | solution.py:525
